TPU v7x, 512 devices: a whole 4x8x8 slice. The times are simulated.
512 devices in a mesh: row: 16 (over z, core), col: 32 (over x, y).
Axes of the slice: x: 4, y: 8, z: 8, core: 2. Of those that a mesh axis runs over, the one named last changes fastest.
Arguments:
- lead: bfloat16 [2, 1024, 2048], P(None, 'row'), may hold values from -0.5 to 28, as said below
- panel: float32 [8192, 2048], P(('row', 'col')), may hold values from -6 to 6
- row_present: int32 [64], replicated, may hold values 0 or 1
- trailing: float32 [8192, 8192], P('row', 'col'), may hold values from -6 to 6
Outputs:
- updated: float32 [8192, 8192], P('row', 'col')
- factor_rows: bfloat16 [8192, 2048], P(('row', 'col'))
Inputs may be any that keep to these rules, and one draw needn't show every extreme that they name: `lead`: the two halves stacked row after row form a symmetric positive definite matrix of order 2048.
All inputs are finite; a program needn't handle non-finite values.
Results may differ from a plain program's by a relative error of at most 0.0013.
Values may be sent and summed in bfloat16 or wider, within the bound.
A program may use at most 128 MiB of HBM per device.

v0:
```python
import jax
import jax.numpy as jnp
from jax import lax
from jax.sharding import PartitionSpec as P

TILE = 128


def spread_2(block, axis, holder):
    block = jnp.where(lax.axis_index(axis) == holder, block, jnp.zeros_like(block))
    return lax.psum(block, axis)


def solve_right(factor, right_side):
    return lax.linalg.triangular_solve(
        factor, right_side, left_side=False, lower=True, transpose_a=True
    )


def contract(left_rows, right_rows):
    return lax.dot_general(
        left_rows, right_rows, (((1,), (1,)), ((), ())), preferred_element_type=jnp.float32
    )


def spread(factor_block):
    row_block = lax.all_gather(factor_block, "col", axis=0, tiled=True)
    row_dev = row_block.shape[0]
    col_dev = row_dev * lax.axis_size("row") // lax.axis_size("col")
    column_index = lax.axis_index("col")
    owner_row = column_index * col_dev // row_dev
    offset = column_index * col_dev - owner_row * row_dev
    whole_block = spread_2(row_block, "row", owner_row)
    column_block = lax.dynamic_slice_in_dim(whole_block, offset, col_dev, 0)
    return (row_block, column_block)


def on_device(lead, panel, row_present, trailing):
    half_width = lead.shape[2] // 2
    first_raw = lax.all_gather(lead[0, :, :half_width], "row", axis=0, tiled=True)
    first_factor = jnp.linalg.cholesky(first_raw.astype(jnp.float32))
    coupling_mine = solve_right(first_factor, lead[1, :, :half_width].astype(jnp.float32)).astype(
        jnp.bfloat16
    )
    panel_count = panel.shape[0]
    first_row = (lax.axis_index("row") * lax.axis_size("col") + lax.axis_index("col")) * panel_count
    tile_of = (first_row + jnp.arange(panel_count, dtype=jnp.int32)) // TILE
    tile_hits = tile_of[:, None] == jnp.arange(row_present.shape[0], dtype=jnp.int32)[None, :]
    present = jnp.sum(jnp.where(tile_hits, row_present[None, :], 0), axis=1).astype(jnp.float32)
    masked = panel * present[:, None]
    first_cols = solve_right(first_factor, masked[:, :half_width]).astype(jnp.bfloat16)
    coupling_all = lax.all_gather(coupling_mine, "row", axis=0, tiled=True)
    schur_mine = lead[1, :, half_width:].astype(jnp.float32) - contract(coupling_mine, coupling_all)
    schur_block = lax.all_gather(schur_mine, "row", axis=0, tiled=True)
    second_factor = jnp.linalg.cholesky(schur_block)
    remainder = masked[:, half_width:] - contract(first_cols, coupling_all)
    second_cols = solve_right(second_factor, remainder).astype(jnp.bfloat16)
    factor_rows = jnp.concatenate([first_cols, second_cols], axis=1)
    rows_all, cols_all = spread(factor_rows)
    updated = trailing - contract(rows_all, cols_all)
    return (updated, factor_rows)


def solution(mesh):
    in_specs = (P(None, "row", None), P(("row", "col"), None), P(), P("row", "col"))
    out_specs = (P("row", "col"), P(("row", "col"), None))
    return jax.shard_map(
        on_device, mesh=mesh, in_specs=in_specs, out_specs=out_specs, check_vma=False
    )
```

profile of v0, /device:TPU:1, one launch (start us, length us, event | category | flops | bytes accessed | tf_op | source)
XLA Modules:
  0.0 1030.3 jit_solution(2442398873901692426)
XLA Ops:
  9.0 50.8 %all-gather.12.cloned.1.call-done = bf16[1,1024,1024]{2,1,0:T(8,128)(2,1)} async-done(((bf16[1,64,1024]{2,1,0:T(8,128)(2,1)}), bf16[1,1024,1024]{2,1,0:T(8,128)(2,1)}) %all-gather.12.cloned.1.call-update) | async-done | bytes 2097168 | tf_op jit(solution)/shard_map/all_gather | solution.py:40
  59.8 2.9 copy.14
  65.1 5.3 copy.15
  70.4 2.9 fusion.1
  75.2 11.7 %cholesky.619 = f32[128,128]{1,0:T(8,128)S(1)} custom-call(f32[128,128]{1,0:T(8,128)S(1)} %cholesky.911), custom_call_target="Cholesky" | custom-call | tf_op jit(solution)/shard_map/jit(cholesky)/cholesky | solution.py:41
  89.5 9.8 custom-call.59
  103.2 11.7 %cholesky.638 = f32[128,128]{1,0:T(8,128)S(1)} custom-call(f32[128,128]{1,0:T(8,128)S(1)} %cholesky.915), custom_call_target="Cholesky" | custom-call | tf_op jit(solution)/shard_map/jit(cholesky)/cholesky | solution.py:41
  115.6 10.0 custom-call.60
  128.9 11.7 %cholesky.659 = f32[128,128]{1,0:T(8,128)S(1)} custom-call(f32[128,128]{1,0:T(8,128)S(1)} %cholesky.920), custom_call_target="Cholesky" | custom-call | tf_op jit(solution)/shard_map/jit(cholesky)/cholesky | solution.py:41
  141.3 9.8 custom-call.61
  154.6 11.9 %cholesky.678 = f32[128,128]{1,0:T(8,128)S(1)} custom-call(f32[128,128]{1,0:T(8,128)S(1)} %cholesky.925), custom_call_target="Cholesky" | custom-call | tf_op jit(solution)/shard_map/jit(cholesky)/cholesky | solution.py:41
  167.1 9.8 custom-call.62
  180.4 11.7 %cholesky.697 = f32[128,128]{1,0:T(8,128)S(1)} custom-call(f32[128,128]{1,0:T(8,128)S(1)} %cholesky.930), custom_call_target="Cholesky" | custom-call | tf_op jit(solution)/shard_map/jit(cholesky)/cholesky | solution.py:41
  192.8 9.8 custom-call.63
  206.4 11.7 %cholesky.716 = f32[128,128]{1,0:T(8,128)S(1)} custom-call(f32[128,128]{1,0:T(8,128)S(1)} %cholesky.935), custom_call_target="Cholesky" | custom-call | tf_op jit(solution)/shard_map/jit(cholesky)/cholesky | solution.py:41
  218.7 9.8 custom-call.64
  231.5 11.7 %cholesky.735 = f32[128,128]{1,0:T(8,128)S(1)} custom-call(f32[128,128]{1,0:T(8,128)S(1)} %cholesky.940), custom_call_target="Cholesky" | custom-call | tf_op jit(solution)/shard_map/jit(cholesky)/cholesky | solution.py:41
  243.9 9.9 custom-call.65
  256.4 11.7 %cholesky.752 = f32[128,128]{1,0:T(8,128)S(1)} custom-call(f32[128,128]{1,0:T(8,128)S(1)} %convolution_subtract_fusion.16), custom_call_target="Cholesky" | custom-call | tf_op jit(solution)/shard_map/jit(cholesky)/cholesky | solution.py:41
  278.4 4.8 select_select_fusion.1
  283.2 23.0 %while.5 = (s32[]{:T(128)}, f32[1024,1024]{1,0:T(8,128)}, s32[8,2]{0,1:T(2,128)S(1)}, f32[8,128,128]{2,1,0:T(8,128)S(1)}, s32[]{:T(128)}) while((s32[]{:T(128)}, f32[1024,1024]{1,0:T(8,128)}, s32[8,2]{0,1:T(2,128)S(1)}, f32[8,128,128]{2,1,0:T(8,128)S(1)}, s32[]{:T(128)}) %tuple.138), condition=%wide.while_cond, body=%wide.while_body.sunk | while | flops 2 | bytes 131189 | solution.py:15
  306.2 78.6 %custom-call.66 = f32[8,128,128]{1,2,0:T(8,128)S(1)} custom-call(f32[8,128,128]{2,1,0:T(8,128)S(1)} %get-tuple-element.26), custom_call_target="InvertDiagBlocksLowerTriangular" | custom-call | tf_op jit(solution)/shard_map/triangular_solve/custom-call.7 | solution.py:15
  396.8 41.4 %all-gather.6.cloned.1.call-done = bf16[1024,1024]{1,0:T(8,128)(2,1)} async-done(((bf16[64,1024]{1,0:T(8,128)(2,1)}), bf16[1024,1024]{1,0:T(8,128)(2,1)}) %all-gather.6.cloned.1.call-update) | async-done | bytes 2097168 | tf_op jit(solution)/shard_map/all_gather | solution.py:52
  438.2 3.2 convolution_subtract_fusion.7
  453.0 32.4 %all-gather.8.cloned.1.call-done = f32[1024,1024]{1,0:T(8,128)} async-done(((f32[64,1024]{1,0:T(8,128)}), f32[1024,1024]{1,0:T(8,128)}) %all-gather.8.cloned.1.call-update) | async-done | bytes 4194320 | tf_op jit(solution)/shard_map/all_gather | solution.py:54
  485.5 5.7 copy.16
  491.2 4.4 fusion
  497.6 11.7 %cholesky.767 = f32[128,128]{1,0:T(8,128)S(1)} custom-call(f32[128,128]{1,0:T(8,128)S(1)} %cholesky.944), custom_call_target="Cholesky" | custom-call | tf_op jit(solution)/shard_map/jit(cholesky)/cholesky | solution.py:55
  511.8 9.8 custom-call.67
  525.6 11.9 %cholesky.786 = f32[128,128]{1,0:T(8,128)S(1)} custom-call(f32[128,128]{1,0:T(8,128)S(1)} %cholesky.948), custom_call_target="Cholesky" | custom-call | tf_op jit(solution)/shard_map/jit(cholesky)/cholesky | solution.py:55
  538.1 9.8 custom-call.68
  551.2 11.7 %cholesky.807 = f32[128,128]{1,0:T(8,128)S(1)} custom-call(f32[128,128]{1,0:T(8,128)S(1)} %cholesky.953), custom_call_target="Cholesky" | custom-call | tf_op jit(solution)/shard_map/jit(cholesky)/cholesky | solution.py:55
  563.6 9.8 custom-call.69
  576.9 11.9 %cholesky.826 = f32[128,128]{1,0:T(8,128)S(1)} custom-call(f32[128,128]{1,0:T(8,128)S(1)} %cholesky.958), custom_call_target="Cholesky" | custom-call | tf_op jit(solution)/shard_map/jit(cholesky)/cholesky | solution.py:55
  589.5 9.8 custom-call.70
  602.7 11.7 %cholesky.845 = f32[128,128]{1,0:T(8,128)S(1)} custom-call(f32[128,128]{1,0:T(8,128)S(1)} %cholesky.963), custom_call_target="Cholesky" | custom-call | tf_op jit(solution)/shard_map/jit(cholesky)/cholesky | solution.py:55
  615.1 10.2 custom-call.71
  628.7 11.7 %cholesky.864 = f32[128,128]{1,0:T(8,128)S(1)} custom-call(f32[128,128]{1,0:T(8,128)S(1)} %cholesky.968), custom_call_target="Cholesky" | custom-call | tf_op jit(solution)/shard_map/jit(cholesky)/cholesky | solution.py:55
  641.0 9.8 custom-call.72
  653.8 11.7 %cholesky.883 = f32[128,128]{1,0:T(8,128)S(1)} custom-call(f32[128,128]{1,0:T(8,128)S(1)} %cholesky.973), custom_call_target="Cholesky" | custom-call | tf_op jit(solution)/shard_map/jit(cholesky)/cholesky | solution.py:55
  666.2 9.8 custom-call.73
  678.6 11.7 %cholesky.900 = f32[128,128]{1,0:T(8,128)S(1)} custom-call(f32[128,128]{1,0:T(8,128)S(1)} %convolution_subtract_fusion.15), custom_call_target="Cholesky" | custom-call | tf_op jit(solution)/shard_map/jit(cholesky)/cholesky | solution.py:55
  701.2 4.8 select_select_fusion
  706.0 23.0 %while.6 = (s32[]{:T(128)}, f32[1024,1024]{1,0:T(8,128)}, s32[8,2]{0,1:T(2,128)S(1)}, f32[8,128,128]{2,1,0:T(8,128)S(1)}, s32[]{:T(128)}) while((s32[]{:T(128)}, f32[1024,1024]{1,0:T(8,128)}, s32[8,2]{0,1:T(2,128)S(1)}, f32[8,128,128]{2,1,0:T(8,128)S(1)}, s32[]{:T(128)}) %tuple.154), condition=%wide.while_cond.clone, body=%wide.while_body.clone.sunk | while | flops 2 | bytes 131189 | solution.py:15
  729.0 78.6 %custom-call.74 = f32[8,128,128]{1,2,0:T(8,128)S(1)} custom-call(f32[8,128,128]{2,1,0:T(8,128)S(1)} %get-tuple-element.27), custom_call_target="InvertDiagBlocksLowerTriangular" | custom-call | tf_op jit(solution)/shard_map/triangular_solve/custom-call.7 | solution.py:15
  818.9 77.3 %all-gather.10.cloned.1.call-done = bf16[512,2048]{1,0:T(8,128)(2,1)} async-done(((bf16[16,2048]{1,0:T(8,128)(2,1)}), bf16[512,2048]{1,0:T(8,128)(2,1)}) %all-gather.10.cloned.1.call-update) | async-done | bytes 2097168 | tf_op jit(solution)/shard_map/all_gather | solution.py:27
  897.7 123.1 %all-reduce.3.cloned.1.call-done = bf16[512,2048]{1,0:T(8,128)(2,1)} async-done(((bf16[512,2048]{1,0:T(8,128)(2,1)}), bf16[512,2048]{1,0:T(8,128)(2,1)}) %all-reduce.3.cloned.1.call-update) | async-done | bytes 2097168 | tf_op jit(solution)/shard_map/psum | solution.py:11
  1020.8 2.8 convolution_subtract_fusion
  (214 shorter events, 160.4 us)
Async XLA Ops:
  7.2 52.7 %all-gather.12.cloned.1.call-start = ((), (), s32[]{:S(2)}) async-start(), calls=%async_computation.4 | async-start | bytes 2228224 | tf_op jit(solution)/shard_map/all_gather | solution.py:40
  8.9 429.3 %all-gather.6.cloned.1.call-start = ((), (), s32[]{:S(2)}) async-start(), calls=%async_computation | async-start | bytes 2228224 | tf_op jit(solution)/shard_map/all_gather | solution.py:52
  73.3 1.9 copy-start.1
  306.2 135.3 %copy-start.7 = (s32[64]{0:T(128)S(1)}, s32[64]{0:T(128)}, u32[]{:S(2)}) copy-start(s32[64]{0:T(128)} %param.9) | copy-start | bytes 772
  306.2 135.5 %copy-start.5 = (f32[16,2048]{1,0:T(8,128)S(1)}, f32[16,2048]{1,0:T(8,128)}, u32[]{:S(2)}) copy-start(f32[16,2048]{1,0:T(8,128)} %param.8) | copy-start | bytes 393220
  396.1 0.6 copy-start.4
  396.8 88.7 %all-gather.8.cloned.1.call-start = ((), (), s32[]{:S(2)}) async-start(), calls=%async_computation.1 | async-start | bytes 4456448 | tf_op jit(solution)/shard_map/all_gather | solution.py:54
  438.2 14.1 %copy-start.2 = (bf16[1024,1024]{1,0:T(8,128)(2,1)S(1)}, bf16[1024,1024]{1,0:T(8,128)(2,1)}, u32[]{:S(2)}) copy-start(bf16[1024,1024]{1,0:T(8,128)(2,1)} %all-gather.6.cloned.1.call-done) | copy-start | bytes 6291460
  441.5 454.7 %all-gather.10.cloned.1.call-start = ((), (), s32[]{:S(2)}) async-start(), calls=%async_computation.2 | async-start | bytes 2162688 | tf_op jit(solution)/shard_map/all_gather | solution.py:27
  495.6 1.9 copy-start
  813.0 207.8 %copy-start.6 = (f32[512,256]{1,0:T(8,128)S(1)}, f32[512,256]{1,0:T(8,128)}, u32[]{:S(2)}) copy-start(f32[512,256]{1,0:T(8,128)} %param.10) | copy-start | bytes 1572868
  818.8 202.0 %all-reduce.3.cloned.1.call-start = ((), (), s32[]{:S(2)}) async-start(), calls=%async_computation.3 | async-start | bytes 4194304 | tf_op jit(solution)/shard_map/psum | solution.py:11
  896.2 124.6 %copy-start.3 = (bf16[512,2048]{1,0:T(8,128)(2,1)S(1)}, bf16[512,2048]{1,0:T(8,128)(2,1)}, u32[]{:S(2)}) copy-start(bf16[512,2048]{1,0:T(8,128)(2,1)} %all-gather.10.cloned.1.call-done) | copy-start | bytes 6291460
Sparse Core Ops, SparseCore 0:
  10.7 49.0 all-gather.11
  396.9 41.2 all-gather.5
  441.6 43.8 all-gather.7
  818.9 77.1 all-gather.9
  898.4 122.3 all-reduce.2
where the time goes:
time: 1040 us; the launch traced here: 1030 us
  other arithmetic  525 us (50%)
  waiting for transfers between devices  325 us (31%)
  matrix products  85.2 us (8%)
  local copies, waits for them, and re-layouts  69.3 us (7%)
  between operations  24.6 us (2%)
    another operation x31, other arithmetic, on_device(): second_factor = jnp.linalg.cholesky(schur_block)  173 us
    another operation x30, other arithmetic, on_device(): first_factor = jnp.linalg.cholesky(first_raw.astype(jnp.float32))  172 us
    another operation x5, other arithmetic, solve_right(): lax.linalg.triangular_solve(factor, right_side, left_side=False, lower=Tr...  167 us
    psum x1, waiting for transfers between devices, spread_2(): return lax.psum(block, axis)  123 us
    all_gather x1, waiting for transfers between devices, spread(): row_block = lax.all_gather(factor_block, 'col', axis=0, tiled=True)  77.3 us
    all_gather x1, waiting for transfers between devices, on_device(): lax.all_gather(lead[0, :, :half_width], 'row', axis=0, tiled=True)  50.8 us
    another operation x52, local copies, waits for them, and re-layouts, solve_right(): lax.linalg.triangular_solve(factor, right_side, left_side=False, lower=Tr...  45.7 us
    all_gather x1, waiting for transfers between devices, on_device(): coupling_all = lax.all_gather(coupling_mine, 'row', axis=0, tiled=True)  41.4 us
  transfers between devices with their start and end apart: 5, of which 5 were waited for; matrix products, arithmetic and copies ran while one was open for 1% of the time, Pallas kernels for 0%

commit v1 on v0

v1 whole, which is shorter than its diff:
```python
import jax
import jax.numpy as jnp
from jax import lax
from jax.experimental import pallas as pl
from jax.experimental.pallas import tpu as pltpu
from jax.sharding import PartitionSpec as P

TILE = 128
F32 = jnp.float32
BF16 = jnp.bfloat16


def lane_cast(x, c):
    return jnp.broadcast_to(x[:, c : c + 1], (8, 128))


def sub_cast(x, j):
    return jnp.broadcast_to(x[j : j + 1, :], (8, 128))


def tree(xs):
    while len(xs) > 1:
        xs = [xs[i] + xs[i + 1] if i + 1 < len(xs) else xs[i] for i in range(0, len(xs), 2)]
    return xs[0]


def factor128(rows):
    lane = lax.broadcasted_iota(jnp.int32, (8, 128), 1)
    sub = lax.broadcasted_iota(jnp.int32, (8, 128), 0)
    rows = list(rows)
    out = []
    for k in range(16):
        c0 = 8 * k
        inside = (lane >= c0) & (lane < c0 + 8)
        casts = {r: [lane_cast(rows[r], c0 + c) for c in range(8)] for r in range(k, 16)}
        cols = list(casts[k])
        forward = jnp.where(inside, jnp.where(lane - c0 == sub, 1.0, 0.0), rows[k])
        full = forward
        recips = jnp.zeros((8, 128), F32)
        for j in range(8):
            recip = 1.0 / sub_cast(cols[j], j)
            mult = cols[j] * recip
            mult_full = jnp.where(sub == j, 0.0, mult)
            mult_fwd = jnp.where(sub > j, mult, 0.0)
            for c in range(j + 1, 8):
                cols[c] = cols[c] - mult_full * sub_cast(cols[c], j)
            full = full - mult_full * sub_cast(full, j)
            forward = forward - mult_fwd * sub_cast(forward, j)
            recips = jnp.where(sub == j, recip, recips)
        full = full * recips
        out.append(jnp.where(lane < c0 + 8, forward * lax.sqrt(recips), 0.0))
        pivots = [sub_cast(full, c) for c in range(8)]
        for r in range(k + 1, 16):
            rows[r] = jnp.where(inside, 0.0, rows[r]) - tree([casts[r][c] * pivots[c] for c in range(8)])
    return out


def split(x):
    hi = x.astype(BF16)
    return hi, (x - hi.astype(F32)).astype(BF16)


def split_outside(x):
    hi = lax.reduce_precision(x, 8, 7)
    return hi.astype(BF16), (x - hi).astype(BF16)


NN = (((1,), (0,)), ((), ()))
NT = (((1,), (1,)), ((), ()))


def dot(a, b, dims):
    return lax.dot_general(a, b, dims, preferred_element_type=F32)


def dot3(a, b, dims):
    return dot(a[0], b[0], dims) + (dot(a[0], b[1], dims) + dot(a[1], b[0], dims))


def inverse_factor_kernel(s_ref, x_ref, inv_ref, top_hi, top_lo, left_hi, left_lo):
    n = s_ref.shape[0]
    blocks = n // 128
    x_ref[...] = s_ref[...]
    column = lax.broadcasted_iota(jnp.int32, (128, n), 1)

    def step(j, carry):
        r0 = pl.multiple_of(j * 128, 128)
        here = pl.ds(r0, 128)
        rows = [x_ref[pl.ds(r0 + 8 * k, 8), here] for k in range(16)]
        for k, row in enumerate(factor128(rows)):
            inv_ref[8 * k : 8 * k + 8, :] = row
        inv = inv_ref[...]
        inv_parts = split(inv)
        top = dot3(inv_parts, split(x_ref[here, :]), NN)
        hi, lo = split(top)
        top_hi[...] = hi
        top_lo[...] = lo
        inv_hi, inv_lo = inv_parts
        top_hi[:, here] = inv_hi
        top_lo[:, here] = inv_lo
        left = dot3(split(x_ref[:, here]), inv_parts, NT)
        hi, lo = split(left)
        left_hi[...] = hi
        left_lo[...] = lo
        x_ref[here, :] = jnp.where(column < r0, top, 0.0)
        x_ref[here, here] = inv

        def below(i, inner):
            i0 = pl.multiple_of(i * 128, 128)
            at = pl.ds(i0, 128)
            take = dot3((left_hi[at, :], left_lo[at, :]), (top_hi[...], top_lo[...]), NN)
            x_ref[at, here] = jnp.zeros((128, 128), F32)
            x_ref[at, :] = x_ref[at, :] - take
            return inner

        lax.fori_loop(j + 1, blocks, below, 0)
        return carry

    lax.fori_loop(0, blocks, step, 0)


def inverse_factor(s):
    n = s.shape[0]
    return pl.pallas_call(
        inverse_factor_kernel,
        out_shape=jax.ShapeDtypeStruct((n, n), F32),
        in_specs=[pl.BlockSpec(memory_space=pltpu.VMEM)],
        out_specs=pl.BlockSpec(memory_space=pltpu.VMEM),
        scratch_shapes=[
            pltpu.VMEM((128, 128), F32),
            pltpu.VMEM((128, n), BF16),
            pltpu.VMEM((128, n), BF16),
            pltpu.VMEM((n, 128), BF16),
            pltpu.VMEM((n, 128), BF16),
        ],
        compiler_params=pltpu.CompilerParams(vmem_limit_bytes=40 << 20),
        cost_estimate=pl.CostEstimate(flops=40_000_000_000, bytes_accessed=8 << 20, transcendentals=0),
    )(s)


def on_device(lead, panel, row_present, trailing):
    half = lead.shape[2] // 2
    rows_n, cols_n = lax.axis_size("row"), lax.axis_size("col")
    row_id, col_id = lax.axis_index("row"), lax.axis_index("col")
    lead_all = gather_lead(lead, half)

    count = panel.shape[0]
    first_row = (row_id * cols_n + col_id) * count
    tile_of = (first_row + jnp.arange(count, dtype=jnp.int32)) // TILE
    hits = tile_of[:, None] == jnp.arange(row_present.shape[0], dtype=jnp.int32)[None, :]
    present = jnp.sum(jnp.where(hits, row_present[None, :], 0), axis=1).astype(F32)
    pieces = jnp.stack(split_outside(panel * present[:, None]))
    row_pieces = lax.all_gather(pieces, "col", axis=1, tiled=True)
    per_col = trailing.shape[1] // count
    pairs = []
    for r in range(rows_n):
        for c in range(cols_n):
            owner = c * per_col + r
            pairs.append((owner, r * cols_n + c))
    col_pieces = lax.ppermute(pieces, ("row", "col"), pairs)
    col_pieces = lax.all_gather(col_pieces, "row", axis=1, tiled=True)

    x1 = inverse_factor(lead_all[0].astype(F32))
    x1_parts = split_outside(x1)
    below = lead_all[1]
    coupling = (dot(below, x1_parts[0], NT) + dot(below, x1_parts[1], NT)).astype(BF16)
    schur = lead_all[2].astype(F32) - dot(coupling, coupling, NT)
    x2_parts = split_outside(inverse_factor(schur))

    def solve(parts):
        left = (parts[0, :, :half], parts[1, :, :half])
        first = dot3(left, x1_parts, NT).astype(BF16)
        right = parts[0, :, half:].astype(F32) + parts[1, :, half:].astype(F32)
        rest = split_outside(right - dot(first, coupling, NT))
        second = dot3(rest, x2_parts, NT).astype(BF16)
        return jnp.concatenate([first, second], axis=1)

    rows_all = solve(row_pieces)
    cols_all = solve(col_pieces)
    updated = trailing - dot(rows_all, cols_all, NT)
    factor_rows = lax.dynamic_slice_in_dim(rows_all, col_id * count, count, 0)
    return (updated, factor_rows)


def gather_lead(lead, half):
    out = []
    for which in (lead[0, :, :half], lead[1, :, :half], lead[1, :, half:]):
        out.append(lax.all_gather(which, "row", axis=0, tiled=True))
    return out


def solution(mesh):
    in_specs = (P(None, "row", None), P(("row", "col"), None), P(), P("row", "col"))
    out_specs = (P("row", "col"), P(("row", "col"), None))
    return jax.shard_map(
        on_device, mesh=mesh, in_specs=in_specs, out_specs=out_specs, check_vma=False
    )
```

time: 1040 us -> 305 us (0.29)
  other arithmetic: 525 us -> 5.2 us
  waiting for transfers between devices: 325 us -> 124 us
  Pallas kernels: 0 us -> 106 us
  local copies, waits for them, and re-layouts: 69.3 us -> 10.9 us
  matrix products: 85.2 us -> 36.2 us
  between operations: 24.6 us -> 14.1 us
    another operation x66 -> x2, other arithmetic: 512 us -> 1.01 us  [on_device(): pieces = jnp.stack(split_outside(panel * present[:, None]))]
    psum x1 -> x0, waiting for transfers between devices: 123 us -> none  [spread_2(): return lax.psum(block, axis)]
    pallas_call x0 -> x2, Pallas kernels: none -> 106 us  [inverse_factor(): pl.pallas_call(inverse_factor_kernel, out_shape=jax.ShapeDtypeStruct((n,...]
    all_gather x4 -> x5, waiting for transfers between devices: 202 us -> 121 us  [the longest x3 64 us: gather_lead(): out.append(lax.all_gather(which, 'row', axis=0, tiled=True))]
    another operation x73 -> x0, matrix products: 78.6 us -> none  [the longest x45 32 us: solve_right(): lax.linalg.triangular_solve(factor, right_side, left_side=False, lower=Tr...]
    another operation x68 -> x0, local copies, waits for them, and re-layouts: 50.8 us -> none  [the longest x52 45.7 us: solve_right(): lax.linalg.triangular_solve(factor, right_side, left_side=False, lower=Tr...]
    dot_general x3 -> x18, matrix products: 6.62 us -> 36.2 us  [dot(): return lax.dot_general(a, b, dims, preferred_element_type=F32)]
  transfers between devices with their start and end apart: 5 -> 6, of which waited for: 5 -> 4; matrix products, arithmetic and copies ran while one was open for 1% -> 9% of each run, Pallas kernels for 0% -> 35%
where the time goes in v1:
time: 305 us; the launch traced here: 303 us
  waiting for transfers between devices  124 us (41%)
  Pallas kernels  106 us (35%)
  matrix products  36.2 us (12%)
  between operations  14.1 us (5%)
  local copies, waits for them, and re-layouts  10.9 us (4%)
  starting transfers between devices  5.8 us (2%)
  other arithmetic  5.2 us (2%)
    pallas_call x2, Pallas kernels, inverse_factor(): pl.pallas_call(inverse_factor_kernel, out_shape=jax.ShapeDtypeStruct((n,...  106 us
    all_gather x3, waiting for transfers between devices, gather_lead(): out.append(lax.all_gather(which, 'row', axis=0, tiled=True))  64 us
    all_gather x1, waiting for transfers between devices, on_device(): row_pieces = lax.all_gather(pieces, 'col', axis=1, tiled=True)  56.5 us
    dot_general x18, matrix products, dot(): return lax.dot_general(a, b, dims, preferred_element_type=F32)  36.2 us
    unnamed x34, local copies, waits for them, and re-layouts  9.09 us
  transfers between devices with their start and end apart: 6, of which 4 were waited for; matrix products, arithmetic and copies ran while one was open for 9% of the time, Pallas kernels for 35%

profile of v1, /device:TPU:1, one launch (start us, length us, event | category | flops | bytes accessed | tf_op | source)
XLA Modules:
  0.0 302.9 jit_solution(11557028054391800462)
XLA Ops:
  7.2 0.0 all-gather.13.cloned.1.call-start
  7.2 1.8 fusion.34
  9.0 0.0 all-gather.15.cloned.1.call-start
  9.1 0.7 all-gather.15.cloned.1.call-update
  9.8 0.7 all-gather.17.cloned.1.call-update
  10.6 0.8 select_reduce_fusion
  11.4 1.0 fusion.29
  12.5 5.6 %collective-permute-start = (bf16[2,16,2048]{2,1,0:T(8,128)(2,1)S(1)}, bf16[2,16,2048]{2,1,0:T(8,128)(2,1)S(1)}, u32[]{:S(2)}, u32[]{:S(2)}) collective-permute-start(bf16[2,16,2048]{2,1,0:T(8,128)(2,1)S(1)} %pad_maximum_fusion.4), channel_id=1, source_target_pairs={{0,0},{16,1},{32,2},{48,3},{64,4},{80,5},{96,6},{112,7},{128,8},{1... | collective-permute-start | bytes 393224 | tf_op jit(solution)/shard_map/ppermute | solution.py:160
  18.1 1.9 collective-permute-done
  20.0 0.7 copy-done.13
  20.7 0.0 all-gather.9.cloned.1.call-start
  20.7 0.5 all-gather.9.cloned.1.call-update
  21.3 38.8 %all-gather.13.cloned.1.call-done = bf16[1,1024,1024]{2,1,0:T(8,128)(2,1)} async-done(((bf16[1,64,1024]{2,1,0:T(8,128)(2,1)}), bf16[1,1024,1024]{2,1,0:T(8,128)(2,1)}) %all-gather.13.cloned.1.call-update) | async-done | bytes 2097168 | tf_op jit(solution)/shard_map/all_gather | solution.py:188
  60.1 2.0 bitcast_convert_fusion.s_ref
  62.1 53.1 %shard_map.59 = f32[1024,1024]{1,0:T(8,128)S(1)} custom-call(f32[1024,1024]{1,0:T(8,128)S(1)} %bitcast_convert_fusion.s_ref), custom_call_target="tpu_custom_call" | custom-call | flops 40000000000 | bytes 8388608 | tf_op jit(solution)/shard_map/pallas_call | solution.py:124
  115.2 2.0 copy-done
  117.3 0.3 reduce-precision_convert_fusion.1
  117.6 4.7 %fusion.6 = f32[1024,1024]{1,0:T(8,128)S(1)} fusion(bf16[1024,1024]{1,0:T(8,128)(2,1)S(1)} %reduce-precision_convert_fusion.1, bf16[1,1024,1024]{2,1,0:T(8,128)(2,1)} %all-gather.15.cloned.1.call-done), kind=kOutput, calls=%fused_computation.18 | convolution fusion | flops 2147483648 | bytes 8388608 | tf_op jit(solution)/shard_map/dot_general | solution.py:73
  122.4 3.8 %fusion.2 = bf16[1024,1024]{1,0:T(8,128)(2,1)} fusion(f32[1024,1024]{1,0:T(8,128)S(1)} %fusion.6, bf16[1,1024,1024]{2,1,0:T(8,128)(2,1)S(1)} %copy-done.15, f32[1024,1024]{1,0:T(8,128)S(1)} %copy-done.1), kind=kOutput, calls=%fused_computation.8 | convolution fusion | flops 2152726528 | bytes 12582912 | tf_op jit(solution)/shard_map/dot_general | solution.py:73
  126.2 25.2 %all-gather.17.cloned.1.call-done = bf16[1,1024,1024]{2,1,0:T(8,128)(2,1)} async-done(((bf16[1,64,1024]{2,1,0:T(8,128)(2,1)}), bf16[1,1024,1024]{2,1,0:T(8,128)(2,1)}) %all-gather.17.cloned.1.call-update) | async-done | bytes 2097168 | tf_op jit(solution)/shard_map/all_gather | solution.py:188
  151.3 5.2 %convert_subtract_fusion.s_ref = f32[1024,1024]{1,0:T(8,128)S(1)} fusion(bf16[1,1024,1024]{2,1,0:T(8,128)(2,1)} %all-gather.17.cloned.1.call-done, bf16[1024,1024]{1,0:T(8,128)(2,1)} %fusion.2), kind=kOutput, calls=%fused_computation.6 | convolution fusion | flops 2149580800 | bytes 8388608 | tf_op jit(solution)/shard_map/dot_general | solution.py:73
  156.6 53.3 %shard_map.60 = f32[1024,1024]{1,0:T(8,128)S(1)} custom-call(f32[1024,1024]{1,0:T(8,128)S(1)} %convert_subtract_fusion.s_ref), custom_call_target="tpu_custom_call" | custom-call | flops 40000000000 | bytes 8388608 | tf_op jit(solution)/shard_map/pallas_call | solution.py:124
  209.9 2.0 copy-done.3
  211.9 0.3 reduce-precision_convert_fusion
  212.2 2.6 fusion.24
  214.9 3.2 %convolution_add_fusion.1 = f32[256,1024]{1,0:T(8,128)S(1)} fusion(f32[256,1024]{1,0:T(8,128)S(1)} %fusion.24, bf16[2,256,2048]{2,1,0:T(8,128)(2,1)S(1)} %copy-done.9, f32[1024,1024]{1,0:T(8,128)} %copy-done), kind=kOutput, calls=%fused_computation.27 | convolution fusion | flops 540278784 | bytes 6815744 | tf_op jit(solution)/shard_map/dot_general | solution.py:73
  218.1 0.7 fusion.10
  218.9 0.8 copy-done.10
  219.7 0.8 reduce-precision_convert_fusion.3
  220.5 0.7 fusion.35
  221.2 0.7 copy-done.4
  221.9 0.8 fusion.19
  222.6 0.8 fusion.9
  223.4 56.5 %all-gather.9.cloned.1.call-done = bf16[2,512,2048]{2,1,0:T(8,128)(2,1)} async-done(((bf16[2,16,2048]{2,1,0:T(8,128)(2,1)}), bf16[2,512,2048]{2,1,0:T(8,128)(2,1)}) %all-gather.9.cloned.1.call-update) | async-done | bytes 4194320 | tf_op jit(solution)/shard_map/all_gather | solution.py:153
  279.9 3.3 %fusion.18 = f32[512,1024]{1,0:T(8,128)S(1)} fusion(bf16[1024,1024]{1,0:T(8,128)(2,1)} %copy-done.6, bf16[2,512,2048]{2,1,0:T(8,128)(2,1)} %all-gather.9.cloned.1.call-done), kind=kOutput, calls=%fused_computation.40 | convolution fusion | flops 1073741824 | bytes 5242880 | tf_op jit(solution)/shard_map/dot_general | solution.py:73
  283.3 1.0 copy-done.14
  284.4 1.3 fusion.17
  285.7 0.3 copy-done.8
  285.9 1.3 add_convert_fusion.1
  287.3 0.3 copy-done.11
  287.5 1.3 bitcast_subtract_fusion
  288.9 0.9 copy-done.5
  289.7 1.3 fusion.21
  291.0 1.3 fusion.25
  292.4 1.4 add_convert_fusion
  293.8 0.6 fusion.27
  294.4 0.4 copy-done.16
  294.9 1.5 fusion.11
  (33 shorter events, 0.2 us)
Async XLA Ops:
  7.2 52.9 %all-gather.13.cloned.1.call-start = ((), (), s32[]{:S(2)}) async-start(), calls=%async_computation.2 | async-start | bytes 2228224 | tf_op jit(solution)/shard_map/all_gather | solution.py:188
  9.0 108.6 %all-gather.15.cloned.1.call-start = ((), (), s32[]{:S(2)}) async-start(), calls=%async_computation.3 | async-start | bytes 2228224 | tf_op jit(solution)/shard_map/all_gather | solution.py:188
  9.8 141.6 %all-gather.17.cloned.1.call-start = ((), (), s32[]{:S(2)}) async-start(), calls=%async_computation.4 | async-start | bytes 2228224 | tf_op jit(solution)/shard_map/all_gather | solution.py:188
  10.5 201.7 %all-gather.11.cloned.1.call-start = ((), (), s32[]{:S(2)}) async-start(), calls=%async_computation.1 | async-start | bytes 2228224 | tf_op jit(solution)/shard_map/all_gather | solution.py:161
  12.4 8.3 %copy-start.12 = (bf16[2,16,2048]{2,1,0:T(8,128)(2,1)}, bf16[2,16,2048]{2,1,0:T(8,128)(2,1)S(1)}, u32[]{:S(2)}) copy-start(bf16[2,16,2048]{2,1,0:T(8,128)(2,1)S(1)} %pad_maximum_fusion.4) | copy-start | bytes 393220
  12.5 7.5 %collective-permute-start = (bf16[2,16,2048]{2,1,0:T(8,128)(2,1)S(1)}, bf16[2,16,2048]{2,1,0:T(8,128)(2,1)S(1)}, u32[]{:S(2)}, u32[]{:S(2)}) collective-permute-start(bf16[2,16,2048]{2,1,0:T(8,128)(2,1)S(1)} %pad_maximum_fusion.4), channel_id=1, source_target_pairs={{0,0},{16,1},{32,2},{48,3},{64,4},{80,5},{96,6},{112,7},{128,8},{1... | collective-permute-start | bytes 393224 | tf_op jit(solution)/shard_map/ppermute | solution.py:160
  20.0 0.7 copy-start.13
  20.7 259.3 %all-gather.9.cloned.1.call-start = ((), (), s32[]{:S(2)}) async-start(), calls=%async_computation | async-start | bytes 4325376 | tf_op jit(solution)/shard_map/all_gather | solution.py:153
  115.2 2.0 copy-start
  117.6 4.8 %copy-start.6 = (bf16[1024,1024]{1,0:T(8,128)(2,1)}, bf16[1024,1024]{1,0:T(8,128)(2,1)S(1)}, u32[]{:S(2)}) copy-start(bf16[1024,1024]{1,0:T(8,128)(2,1)S(1)} %reduce-precision_convert_fusion.1) | copy-start | bytes 6291460
  117.6 4.8 %copy-start.1 = (f32[1024,1024]{1,0:T(8,128)S(1)}, f32[1024,1024]{1,0:T(8,128)}, u32[]{:S(2)}) copy-start(f32[1024,1024]{1,0:T(8,128)} %copy-done) | copy-start | bytes 12582916
  117.6 4.8 %copy-start.15 = (bf16[1,1024,1024]{2,1,0:T(8,128)(2,1)S(1)}, bf16[1,1024,1024]{2,1,0:T(8,128)(2,1)}, u32[]{:S(2)}) copy-start(bf16[1,1024,1024]{2,1,0:T(8,128)(2,1)} %all-gather.15.cloned.1.call-done) | copy-start | bytes 6291460
  209.9 2.0 copy-start.3
  212.2 2.7 copy-start.9
  214.9 3.2 %copy-start.7 = (bf16[1024,1024]{1,0:T(8,128)(2,1)S(1)}, bf16[1024,1024]{1,0:T(8,128)(2,1)}, u32[]{:S(2)}) copy-start(bf16[1024,1024]{1,0:T(8,128)(2,1)} %copy-done.6) | copy-start | bytes 6291460
  218.1 1.6 copy-start.10
  219.7 2.2 copy-start.4
  279.9 3.4 %copy-start.2 = (f32[1024,1024]{1,0:T(8,128)S(1)}, f32[1024,1024]{1,0:T(8,128)}, u32[]{:S(2)}) copy-start(f32[1024,1024]{1,0:T(8,128)} %copy-done) | copy-start | bytes 12582916
  279.9 4.4 %copy-start.14 = (bf16[2,512,2048]{2,1,0:T(8,128)(2,1)S(1)}, bf16[2,512,2048]{2,1,0:T(8,128)(2,1)}, u32[]{:S(2)}) copy-start(bf16[2,512,2048]{2,1,0:T(8,128)(2,1)} %all-gather.9.cloned.1.call-done) | copy-start | bytes 12582916
  284.4 1.6 copy-start.8
  285.9 1.6 copy-start.11
  287.5 2.2 copy-start.5
  293.8 1.1 copy-start.16
Sparse Core Ops, SparseCore 0:
  10.1 49.8 all-gather.12
  62.7 45.1 all-gather.14
  110.1 41.2 all-gather.16
  153.3 41.4 all-gather.10
  197.8 82.0 all-gather.8

commit v2 on v1

--- a/solution.py
+++ b/solution.py
@@ -77,10 +77,14 @@
     return dot(a[0], b[0], dims) + (dot(a[0], b[1], dims) + dot(a[1], b[0], dims))
 
 
-def inverse_factor_kernel(s_ref, x_ref, inv_ref, top_hi, top_lo, left_hi, left_lo):
-    n = s_ref.shape[0]
+def inverse_factor_kernel(s_ref, x_ref, *scratch):
+    x_ref[...] = s_ref[...]
+    invert_in_place(x_ref, *scratch)
+
+
+def invert_in_place(x_ref, inv_ref, top_hi, top_lo, left_hi, left_lo):
+    n = x_ref.shape[0]
     blocks = n // 128
-    x_ref[...] = s_ref[...]
     column = lax.broadcasted_iota(jnp.int32, (128, n), 1)
 
     def step(j, carry):
@@ -119,6 +123,16 @@
     lax.fori_loop(0, blocks, step, 0)
 
 
+def factor_scratch(n):
+    return [
+        pltpu.VMEM((128, 128), F32),
+        pltpu.VMEM((128, n), BF16),
+        pltpu.VMEM((128, n), BF16),
+        pltpu.VMEM((n, 128), BF16),
+        pltpu.VMEM((n, 128), BF16),
+    ]
+
+
 def inverse_factor(s):
     n = s.shape[0]
     return pl.pallas_call(
@@ -126,24 +140,143 @@
         out_shape=jax.ShapeDtypeStruct((n, n), F32),
         in_specs=[pl.BlockSpec(memory_space=pltpu.VMEM)],
         out_specs=pl.BlockSpec(memory_space=pltpu.VMEM),
-        scratch_shapes=[
-            pltpu.VMEM((128, 128), F32),
-            pltpu.VMEM((128, n), BF16),
-            pltpu.VMEM((128, n), BF16),
-            pltpu.VMEM((n, 128), BF16),
-            pltpu.VMEM((n, 128), BF16),
-        ],
+        scratch_shapes=factor_scratch(n),
         compiler_params=pltpu.CompilerParams(vmem_limit_bytes=40 << 20),
         cost_estimate=pl.CostEstimate(flops=40_000_000_000, bytes_accessed=8 << 20, transcendentals=0),
     )(s)
+
+
+ZS, YS, XS = 8, 8, 4
+MESH = pl.DeviceIdType.MESH
+
+
+def lead_kernel(lead_ref, hi_ref, lo_ref, coupling_ref, schur_ref, buf, work, *scratch):
+    factor_refs, (send_sem, recv_sem) = scratch[:5], scratch[5:]
+    row, col = lax.axis_index("row"), lax.axis_index("col")
+    z, core = row // 2, row % 2
+    x, y = col // YS, col % YS
+    half = lead_ref.shape[2] // 2
+
+    peers = []
+    for d in range(1, ZS):
+        peers.append((lax.rem(z + d, ZS) * 2 + core, col))
+    for d in range(1, YS):
+        peers.append((row, x * YS + lax.rem(y + d, YS)))
+    for d in range(1, XS):
+        peers.append((row, lax.rem(x + d, XS) * YS + y))
+    peers.append((z * 2 + 1 - core, col))
+
+    barrier = pltpu.get_barrier_semaphore()
+    for peer in peers:
+        pl.semaphore_signal(barrier, inc=1, device_id=peer, device_id_type=MESH)
+
+    high = pl.ds(pl.multiple_of(x * 16, 16), 16)
+    wide = pl.ds(pl.multiple_of(y * 128, 128), 128)
+    wide_right = pl.ds(pl.multiple_of(half + y * 128, 128), 128)
+    buf[0, z, core, high, wide] = lead_ref[0, high, wide]
+    buf[1, z, core, high, wide] = lead_ref[1, high, wide]
+    buf[2, z, core, high, wide] = lead_ref[1, high, wide_right]
+    pl.semaphore_wait(barrier, len(peers))
+
+    def copies(group, phase, part):
+        first, count = [(0, ZS - 1), (ZS - 1, YS - 1), (ZS + YS - 2, XS - 1), (ZS + YS + XS - 3, 1)][phase]
+        return [
+            pltpu.make_async_remote_copy(
+                src_ref=part,
+                dst_ref=part,
+                send_sem=send_sem.at[group, first + n],
+                recv_sem=recv_sem.at[group, first + n],
+                device_id=peers[first + n],
+                device_id_type=MESH,
+            )
+            for n in range(count)
+        ]
+
+    def phases(group, which):
+        return [
+            copies(group, 0, buf.at[which, z, core, high, wide]),
+            copies(group, 1, buf.at[which, :, core, high, wide]),
+            copies(group, 2, buf.at[which, :, core, high, :]),
+            copies(group, 3, buf.at[which, :, core]),
+        ]
+
+    def start(cs):
+        for c in cs:
+            c.start()
+
+    def wait(cs):
+        for c in cs:
+            c.wait()
+
+    first = phases(0, pl.ds(0, 1))
+    rest = phases(1, pl.ds(1, 2))
+    start(first[0])
+    start(rest[0])
+    wait(first[0])
+    start(first[1])
+    wait(first[1])
+    start(first[2])
+    wait(rest[0])
+    wait(first[2])
+    start(first[3])
+    start(rest[1])
+    wait(first[3])
+    work[...] = buf[0].reshape(work.shape).astype(F32)
+
+    wait(rest[1])
+    start(rest[2])
+    invert_in_place(work, *factor_refs)
+    wait(rest[2])
+    start(rest[3])
+    hi, lo = split(work[...])
+    hi_ref[...] = hi
+    lo_ref[...] = lo
+    wait(rest[3])
+
+    def coupling_rows(i, carry):
+        at = pl.ds(pl.multiple_of(i * 128, 128), 128)
+        left = buf[1, i].reshape(128, half)
+        coupling_ref[at, :] = (dot(left, hi_ref[...], NT) + dot(left, lo_ref[...], NT)).astype(BF16)
+        return carry
+
+    lax.fori_loop(0, half // 128, coupling_rows, 0)
+
+    def schur_rows(i, carry):
+        at = pl.ds(pl.multiple_of(i * 128, 128), 128)
+        schur_ref[at, :] = buf[2, i].reshape(128, half).astype(F32) - dot(coupling_ref[at, :], coupling_ref[...], NT)
+        return carry
+
+    lax.fori_loop(0, half // 128, schur_rows, 0)
+
+
+def lead_factor(lead):
+    half = lead.shape[2] // 2
+    square = (half, half)
+    vmem = pl.BlockSpec(memory_space=pltpu.VMEM)
+    shapes = [(square, BF16), (square, BF16), (square, BF16), (square, F32)]
+    return pl.pallas_call(
+        lead_kernel,
+        out_shape=[jax.ShapeDtypeStruct(s, t) for s, t in shapes],
+        in_specs=[vmem],
+        out_specs=[vmem] * 4,
+        scratch_shapes=[
+            pltpu.VMEM((3, ZS, 2, half // 16, half), BF16),
+            pltpu.VMEM(square, F32),
+            *factor_scratch(half),
+            pltpu.SemaphoreType.DMA((2, ZS + YS + XS - 2)),
+            pltpu.SemaphoreType.DMA((2, ZS + YS + XS - 2)),
+        ],
+        compiler_params=pltpu.CompilerParams(
+            vmem_limit_bytes=48 << 20, collective_id=0, has_side_effects=True
+        ),
+        cost_estimate=pl.CostEstimate(flops=60_000_000_000, bytes_accessed=16 << 20, transcendentals=0),
+    )(lead)
 
 
 def on_device(lead, panel, row_present, trailing):
     half = lead.shape[2] // 2
     rows_n, cols_n = lax.axis_size("row"), lax.axis_size("col")
     row_id, col_id = lax.axis_index("row"), lax.axis_index("col")
-    lead_all = gather_lead(lead, half)
-
     count = panel.shape[0]
     first_row = (row_id * cols_n + col_id) * count
     tile_of = (first_row + jnp.arange(count, dtype=jnp.int32)) // TILE
@@ -160,11 +293,7 @@
     col_pieces = lax.ppermute(pieces, ("row", "col"), pairs)
     col_pieces = lax.all_gather(col_pieces, "row", axis=1, tiled=True)
 
-    x1 = inverse_factor(lead_all[0].astype(F32))
-    x1_parts = split_outside(x1)
-    below = lead_all[1]
-    coupling = (dot(below, x1_parts[0], NT) + dot(below, x1_parts[1], NT)).astype(BF16)
-    schur = lead_all[2].astype(F32) - dot(coupling, coupling, NT)
+    *x1_parts, coupling, schur = lead_factor(lead)
     x2_parts = split_outside(inverse_factor(schur))
 
     def solve(parts):
@@ -182,13 +311,6 @@
     return (updated, factor_rows)
 
 
-def gather_lead(lead, half):
-    out = []
-    for which in (lead[0, :, :half], lead[1, :, :half], lead[1, :, half:]):
-        out.append(lax.all_gather(which, "row", axis=0, tiled=True))
-    return out
-
-
 def solution(mesh):
     in_specs = (P(None, "row", None), P(("row", "col"), None), P(), P("row", "col"))
     out_specs = (P("row", "col"), P(("row", "col"), None))

time: 305 us -> 254 us (0.83)
  waiting for transfers between devices: 124 us -> 2.65 us
  Pallas kernels: 106 us -> 196 us
  matrix products: 36.2 us -> 19.6 us
    pallas_call x0 -> x1, Pallas kernels: none -> 143 us  [lead_factor(): pl.pallas_call(lead_kernel, out_shape=[jax.ShapeDtypeStruct(s, t) for s,...]
    all_gather x3 -> x0, waiting for transfers between devices: 64 us -> none  [gather_lead(): out.append(lax.all_gather(which, 'row', axis=0, tiled=True))]
    all_gather x1, waiting for transfers between devices: 56.5 us -> 0.02 us  [on_device(): row_pieces = lax.all_gather(pieces, 'col', axis=1, tiled=True)]
    pallas_call x2 -> x1, Pallas kernels: 106 us -> 53.3 us  [inverse_factor(): pl.pallas_call(inverse_factor_kernel, out_shape=jax.ShapeDtypeStruct((n,...]
    dot_general x18 -> x15, matrix products: 36.2 us -> 19.6 us  [dot(): return lax.dot_general(a, b, dims, preferred_element_type=F32)]
  transfers between devices with their start and end apart: 6 -> 3, of which waited for: 4 -> 1; matrix products, arithmetic and copies ran while one was open for 9% -> 4% of each run, Pallas kernels for 35% -> 77%
where the time goes in v2:
time: 254 us; the launch traced here: 253 us
  Pallas kernels  196 us (77%)
  matrix products  19.6 us (8%)
  between operations  14.3 us (6%)
  local copies, waits for them, and re-layouts  11.2 us (4%)
  starting transfers between devices  5.69 us (2%)
  other arithmetic  4.16 us (2%)
  waiting for transfers between devices  2.65 us (1%)
    pallas_call x1, Pallas kernels, lead_factor(): pl.pallas_call(lead_kernel, out_shape=[jax.ShapeDtypeStruct(s, t) for s,...  143 us
    pallas_call x1, Pallas kernels, inverse_factor(): pl.pallas_call(inverse_factor_kernel, out_shape=jax.ShapeDtypeStruct((n,...  53.3 us
    dot_general x15, matrix products, dot(): return lax.dot_general(a, b, dims, preferred_element_type=F32)  19.6 us
    unnamed x34, local copies, waits for them, and re-layouts  11.2 us
    ppermute x1, starting transfers between devices, on_device(): col_pieces = lax.ppermute(pieces, ('row', 'col'), pairs)  5.61 us
  transfers between devices with their start and end apart: 3, of which 1 were waited for; matrix products, arithmetic and copies ran while one was open for 4% of the time, Pallas kernels for 77%

profile of v2, /device:TPU:1, one launch (start us, length us, event | category | flops | bytes accessed | tf_op | source)
XLA Modules:
  0.0 253.4 jit_solution(10075850310916871546)
XLA Ops:
  7.2 0.0 all-gather.5.cloned.1.call-start
  7.2 0.8 select_reduce_fusion
  8.1 1.0 fusion.24
  9.1 0.0 copy-start.13
  9.1 5.6 %collective-permute-start = (bf16[2,16,2048]{2,1,0:T(8,128)(2,1)S(1)}, bf16[2,16,2048]{2,1,0:T(8,128)(2,1)S(1)}, u32[]{:S(2)}, u32[]{:S(2)}) collective-permute-start(bf16[2,16,2048]{2,1,0:T(8,128)(2,1)S(1)} %pad_maximum_fusion.4), channel_id=1, source_target_pairs={{0,0},{16,1},{32,2},{48,3},{64,4},{80,5},{96,6},{112,7},{128,8},{1... | collective-permute-start | bytes 393224 | tf_op jit(solution)/shard_map/ppermute | solution.py:293
  14.7 1.9 collective-permute-done
  16.7 0.6 copy-done.14
  17.3 0.0 all-gather.5.cloned.1.call-update
  17.3 0.0 all-gather.3.cloned.1.call-start
  17.4 0.0 copy-done.13
  17.4 0.7 all-gather.3.cloned.1.call-update
  18.1 0.0 copy-start.6
  18.1 1.0 copy-done.6
  19.1 142.5 %shard_map.59 = (bf16[1024,1024]{1,0:T(8,128)(2,1)S(1)}, bf16[1024,1024]{1,0:T(8,128)(2,1)S(1)}, bf16[1024,1024]{1,0:T(8,128)(2,1)}, f32[1024,1024]{1,0:T(8,128)}) custom-call(bf16[2,64,2048]{2,1,0:T(8,128)(2,1)S(1)} %copy-done.6), custom_call_target="tpu_custom_call" | custom-call | flops 60000002048 | bytes 16777216 | tf_op jit(solution)/shard_map/pallas_call | solution.py:257
  161.7 0.0 copy-start.3
  161.7 1.3 copy-done.3
  163.0 2.2 copy-done.7
  165.2 53.3 %shard_map.60 = f32[1024,1024]{1,0:T(8,128)S(1)} custom-call(f32[1024,1024]{1,0:T(8,128)S(1)} %copy-done.7), custom_call_target="tpu_custom_call" | custom-call | flops 40000000000 | bytes 8388608 | tf_op jit(solution)/shard_map/pallas_call | solution.py:138
  218.5 2.0 copy-done
  220.5 1.6 reduce-precision_convert_fusion
  222.1 1.9 fusion.19
  224.1 0.0 copy-done.4
  224.1 0.0 copy-start.10
  224.1 2.0 convolution_add_fusion.1
  226.1 0.8 fusion.5
  226.8 0.8 copy-done.11
  227.7 0.8 reduce-precision_convert_fusion.2
  228.5 0.7 fusion.26
  229.2 0.8 copy-done.1
  230.0 0.8 fusion.14
  230.8 0.8 fusion.4
  231.5 0.0 all-gather.3.cloned.1.call-done
  231.6 2.7 %fusion.13 = f32[512,1024]{1,0:T(8,128)S(1)} fusion(bf16[1024,1024]{1,0:T(8,128)(2,1)S(1)} %get-tuple-element.6, bf16[2,512,2048]{2,1,0:T(8,128)(2,1)} %all-gather.3.cloned.1.call-done), kind=kOutput, calls=%fused_computation.30 | convolution fusion | flops 1073741824 | bytes 5242880 | tf_op jit(solution)/shard_map/dot_general | solution.py:73
  234.3 0.4 copy-done.15
  234.7 1.3 fusion.12
  236.0 0.0 copy-start.12
  236.0 1.3 add_convert_fusion.1
  237.3 0.3 copy-done.12
  237.6 1.3 bitcast_subtract_fusion
  238.9 0.9 copy-done.2
  239.8 1.3 fusion.16
  241.1 0.3 copy-done.9
  241.4 1.3 fusion.20
  242.7 1.3 add_convert_fusion
  244.0 0.0 copy-start.16
  244.0 0.6 fusion.22
  244.6 0.4 copy-done.16
  245.0 1.5 fusion.6
  (18 shorter events, 0.1 us)
Async XLA Ops:
  7.2 215.0 %all-gather.5.cloned.1.call-start = ((), (), s32[]{:S(2)}) async-start(), calls=%async_computation.1 | async-start | bytes 2228224 | tf_op jit(solution)/shard_map/all_gather | solution.py:294
  9.1 8.3 %copy-start.13 = (bf16[2,16,2048]{2,1,0:T(8,128)(2,1)}, bf16[2,16,2048]{2,1,0:T(8,128)(2,1)S(1)}, u32[]{:S(2)}) copy-start(bf16[2,16,2048]{2,1,0:T(8,128)(2,1)S(1)} %pad_maximum_fusion.4) | copy-start | bytes 393220
  9.1 7.5 %collective-permute-start = (bf16[2,16,2048]{2,1,0:T(8,128)(2,1)S(1)}, bf16[2,16,2048]{2,1,0:T(8,128)(2,1)S(1)}, u32[]{:S(2)}, u32[]{:S(2)}) collective-permute-start(bf16[2,16,2048]{2,1,0:T(8,128)(2,1)S(1)} %pad_maximum_fusion.4), channel_id=1, source_target_pairs={{0,0},{16,1},{32,2},{48,3},{64,4},{80,5},{96,6},{112,7},{128,8},{1... | collective-permute-start | bytes 393224 | tf_op jit(solution)/shard_map/ppermute | solution.py:293
  16.7 0.7 copy-start.14
  17.3 214.2 %all-gather.3.cloned.1.call-start = ((), (), s32[]{:S(2)}) async-start(), calls=%async_computation | async-start | bytes 4325376 | tf_op jit(solution)/shard_map/all_gather | solution.py:286
  18.1 1.0 copy-start.6
  161.7 1.3 copy-start.3
  163.0 2.2 copy-start.7
  218.5 2.0 copy-start
  222.1 1.9 copy-start.4
  224.1 2.0 copy-start.10
  226.1 1.6 copy-start.11
  226.1 2.4 copy-start.8
  227.7 2.3 copy-start.1
  231.6 2.7 %copy-start.5 = (bf16[1024,1024]{1,0:T(8,128)(2,1)S(1)}, bf16[1024,1024]{1,0:T(8,128)(2,1)}, u32[]{:S(2)}) copy-start(bf16[1024,1024]{1,0:T(8,128)(2,1)} %copy-done.3) | copy-start | bytes 6291460
  231.6 3.1 %copy-start.15 = (bf16[2,512,2048]{2,1,0:T(8,128)(2,1)S(1)}, bf16[2,512,2048]{2,1,0:T(8,128)(2,1)}, u32[]{:S(2)}) copy-start(bf16[2,512,2048]{2,1,0:T(8,128)(2,1)} %all-gather.3.cloned.1.call-done) | copy-start | bytes 12582916
  236.0 1.6 copy-start.12
  237.6 2.2 copy-start.2
  239.8 1.6 copy-start.9
  244.0 1.1 copy-start.16
Sparse Core Ops, SparseCore 0:
  17.4 63.0 all-gather.4
  84.2 82.0 all-gather.2

commit v3 on v1

v3 whole, which is shorter than its diff:
```python
import jax
import jax.numpy as jnp
from jax import lax
from jax.experimental import pallas as pl
from jax.experimental.pallas import tpu as pltpu
from jax.sharding import PartitionSpec as P

TILE = 128
F32 = jnp.float32
BF16 = jnp.bfloat16


def lane_cast(x, c):
    return jnp.broadcast_to(x[:, c : c + 1], (8, 128))


def sub_cast(x, j):
    return jnp.broadcast_to(x[j : j + 1, :], (8, 128))


def tree(xs):
    while len(xs) > 1:
        xs = [xs[i] + xs[i + 1] if i + 1 < len(xs) else xs[i] for i in range(0, len(xs), 2)]
    return xs[0]


def factor128(rows):
    lane = lax.broadcasted_iota(jnp.int32, (8, 128), 1)
    sub = lax.broadcasted_iota(jnp.int32, (8, 128), 0)
    zero = jnp.zeros((8, 128), F32)
    rows = list(rows)
    out = []
    for k in range(0, 16, 2):
        c0 = 8 * k
        inside = (lane >= c0) & (lane < c0 + 16)
        casts = {r: [lane_cast(rows[r], c0 + c) for c in range(16)] for r in range(k, min(16, k + 4))}
        cols = [[casts[k][c], casts[k + 1][c]] for c in range(16)]
        forward = [jnp.where(inside, jnp.where(lane - c0 - 8 * i == sub, 1.0, 0.0), rows[k + i]) for i in range(2)]
        full = list(forward)
        recips = [zero, zero]
        for j in range(16):
            at, js = j // 8, j % 8
            recip = 1.0 / sub_cast(cols[j][at], js)
            mult = [cols[j][i] * recip for i in range(2)]
            below = [jnp.where(sub > js, mult[i], 0.0) if i == at else mult[i] for i in range(2)]
            mult[at] = jnp.where(sub == js, 0.0, mult[at])
            for c in range(j + 1, 16):
                pivot = sub_cast(cols[c][at], js)
                cols[c] = [cols[c][i] - mult[i] * pivot for i in range(2)]
            pivot = sub_cast(full[at], js)
            full = [full[i] - mult[i] * pivot for i in range(2)]
            pivot = sub_cast(forward[at], js)
            forward = [forward[i] - below[i] * pivot if i >= at else forward[i] for i in range(2)]
            recips[at] = jnp.where(sub == js, recip, recips[at])
        full = [full[i] * recips[i] for i in range(2)]
        for i in range(2):
            out.append(jnp.where(lane < c0 + 8 * i + 8, forward[i] * lax.sqrt(recips[i]), 0.0))
        pivots = [sub_cast(full[c // 8], c % 8) for c in range(16)]
        far = range(k + 4, 16)
        if len(far) > 0:
            step = split(jnp.concatenate([full[r - k] if k <= r < k + 2 else zero for r in range(16)], axis=0))
            take = dot3(split(jnp.concatenate([jnp.where(inside, rows[r], 0.0) for r in far], axis=0)), step, NN)
        for r in range(k + 2, 16):
            kept = jnp.where(inside, 0.0, rows[r])
            if r < k + 4:
                rows[r] = kept - tree([casts[r][c] * pivots[c] for c in range(16)])
            else:
                rows[r] = kept - take[8 * (r - k - 4) : 8 * (r - k - 4) + 8, :]
    return out


def split(x):
    hi = x.astype(BF16)
    return hi, (x - hi.astype(F32)).astype(BF16)


def split_outside(x):
    hi = lax.reduce_precision(x, 8, 7)
    return hi.astype(BF16), (x - hi).astype(BF16)


NN = (((1,), (0,)), ((), ()))
NT = (((1,), (1,)), ((), ()))


def dot(a, b, dims):
    return lax.dot_general(a, b, dims, preferred_element_type=F32)


def dot3(a, b, dims):
    return dot(a[0], b[0], dims) + (dot(a[0], b[1], dims) + dot(a[1], b[0], dims))


def invert_in_place(x_ref, inv_ref, top_hi, top_lo, left_hi, left_lo, before=None):
    n = x_ref.shape[0]
    blocks = n // 128
    column = lax.broadcasted_iota(jnp.int32, (128, n), 1)

    def step(j, carry):
        if before is not None:
            before(j)
        r0 = pl.multiple_of(j * 128, 128)
        here = pl.ds(r0, 128)
        rows = [x_ref[pl.ds(r0 + 8 * k, 8), here] for k in range(16)]
        for k, row in enumerate(factor128(rows)):
            inv_ref[8 * k : 8 * k + 8, :] = row
        inv = inv_ref[...]
        inv_parts = split(inv)
        top = dot3(inv_parts, split(x_ref[here, :]), NN)
        hi, lo = split(top)
        top_hi[...] = hi
        top_lo[...] = lo
        inv_hi, inv_lo = inv_parts
        top_hi[:, here] = inv_hi
        top_lo[:, here] = inv_lo
        left = dot3(split(x_ref[:, here]), inv_parts, NT)
        hi, lo = split(left)
        left_hi[...] = hi
        left_lo[...] = lo
        x_ref[here, :] = jnp.where(column < r0, top, 0.0)
        x_ref[here, here] = inv

        def below(i, inner):
            i0 = pl.multiple_of(i * 128, 128)
            at = pl.ds(i0, 128)
            take = dot3((left_hi[at, :], left_lo[at, :]), (top_hi[...], top_lo[...]), NN)
            x_ref[at, here] = jnp.zeros((128, 128), F32)
            x_ref[at, :] = x_ref[at, :] - take
            return inner

        lax.fori_loop(j + 1, blocks, below, 0)
        return carry

    lax.fori_loop(0, blocks, step, 0)


def factor_scratch(n):
    return [
        pltpu.VMEM((128, 128), F32),
        pltpu.VMEM((128, n), BF16),
        pltpu.VMEM((128, n), BF16),
        pltpu.VMEM((n, 128), BF16),
        pltpu.VMEM((n, 128), BF16),
    ]


ZS = 8
MESH = pl.DeviceIdType.MESH


def neighbours():
    row, col = lax.axis_index("row"), lax.axis_index("col")
    z, core = row // 2, row % 2
    up = (lax.rem(z + 1, ZS) * 2 + core, col)
    down = (lax.rem(z + ZS - 1, ZS) * 2 + core, col)
    return z, core, up, down, (z * 2 + 1 - core, col)


class Ring:
    def __init__(self, block_of, send_sem, recv_sem):
        z, core, up, down, other = neighbours()

        def copy(n, block, peer):
            part = block_of(lax.rem(block + ZS, ZS), core)
            return pltpu.make_async_remote_copy(
                src_ref=part,
                dst_ref=part,
                send_sem=send_sem.at[n],
                recv_sem=recv_sem.at[n],
                device_id=peer,
                device_id_type=MESH,
            )

        self.ups = [copy(n, z - n, up) for n in range(4)]
        self.downs = [copy(4 + n, z + n, down) for n in range(3)]
        self.across = [copy(7 + n, z - n, other) for n in range(5)]
        self.across += [copy(11 + n, z + n, other) for n in range(1, 4)]

    def begin(self):
        self.ups[0].start()
        self.downs[0].start()
        self.across[0].start()

    def advance(self, n):
        self.ups[n].wait_recv()
        if n < 3:
            self.ups[n + 1].start()
            self.downs[n].wait_recv()
        if n < 2:
            self.downs[n + 1].start()
        self.across[1 + n].start()
        if n < 3:
            self.across[5 + n].start()

    def finish(self):
        for c in self.across:
            c.wait()
        for c in self.ups + self.downs:
            c.wait_send()

    def advance_at(self, turns):
        def before(j):
            for n, turn in enumerate(turns):

                @pl.when(j == turn)
                def _():
                    self.advance(n)

        return before


def greet():
    barrier = pltpu.get_barrier_semaphore()
    for peer in neighbours()[2:]:
        pl.semaphore_signal(barrier, inc=1, device_id=peer, device_id_type=MESH)
    return barrier


def lead_kernel(lead_ref, hi_ref, lo_ref, coupling_ref, schur_ref, buf, work, *scratch):
    factor_refs, (send_sem, recv_sem) = scratch[:5], scratch[5:]
    z, core = neighbours()[:2]
    half = lead_ref.shape[2] // 2
    barrier = greet()
    buf[0, z, core] = lead_ref[0, :, :half]
    buf[1, z, core] = lead_ref[1, :, :half]
    buf[2, z, core] = lead_ref[1, :, half:]
    pl.semaphore_wait(barrier, 3)

    first = Ring(lambda b, c: buf.at[pl.ds(0, 1), b, c], send_sem.at[0], recv_sem.at[0])
    rest = Ring(lambda b, c: buf.at[pl.ds(1, 2), b, c], send_sem.at[1], recv_sem.at[1])
    first.begin()
    for n in range(4):
        first.advance(n)
    rest.begin()
    first.finish()
    work[...] = buf[0].reshape(work.shape).astype(F32)
    invert_in_place(work, *factor_refs, before=rest.advance_at((2, 4, 5, 7)))
    hi, lo = split(work[...])
    hi_ref[...] = hi
    lo_ref[...] = lo
    rest.finish()

    wide = 256
    for n in range(half // wide):
        at = slice(n * wide, n * wide + wide)
        depth = (n + 1) * wide
        left = buf[1, :, :, :, :depth].reshape(half, depth)
        coupling_ref[:, at] = (dot(left, hi_ref[at, :depth], NT) + dot(left, lo_ref[at, :depth], NT)).astype(BF16)

    def schur_columns(n, carry):
        at = pl.ds(pl.multiple_of(n * wide, wide), wide)
        block = buf[2, :, :, :, at].reshape(half, wide).astype(F32)
        schur_ref[:, at] = block - dot(coupling_ref[...], coupling_ref[at, :], NT)
        return carry

    lax.fori_loop(0, half // wide, schur_columns, 0)


def lead_factor(lead):
    half = lead.shape[2] // 2
    square = (half, half)
    vmem = pl.BlockSpec(memory_space=pltpu.VMEM)
    shapes = [(square, BF16)] * 3 + [(square, F32)]
    return pl.pallas_call(
        lead_kernel,
        out_shape=[jax.ShapeDtypeStruct(s, t) for s, t in shapes],
        in_specs=[vmem],
        out_specs=[vmem] * 4,
        scratch_shapes=[
            pltpu.VMEM((3, ZS, 2, half // 16, half), BF16),
            pltpu.VMEM(square, F32),
            *factor_scratch(half),
            pltpu.SemaphoreType.DMA((2, 15)),
            pltpu.SemaphoreType.DMA((2, 15)),
        ],
        compiler_params=pltpu.CompilerParams(
            vmem_limit_bytes=48 << 20, collective_id=0, has_side_effects=True
        ),
        cost_estimate=pl.CostEstimate(flops=6_000_000_000, bytes_accessed=16 << 20, transcendentals=0),
    )(lead)


def second_kernel(schur_ref, own_ref, hi_ref, lo_ref, cols_ref, work, *scratch):
    factor_refs, (send_sem, recv_sem) = scratch[:5], scratch[5:]
    z, core = neighbours()[:2]
    barrier = greet()
    cols_ref[z, core] = own_ref[...]
    work[...] = schur_ref[...]
    pl.semaphore_wait(barrier, 3)
    ring = Ring(lambda b, c: cols_ref.at[b, c], send_sem, recv_sem)
    ring.begin()
    invert_in_place(work, *factor_refs, before=ring.advance_at((1, 2, 3, 4)))
    hi, lo = split(work[...])
    hi_ref[...] = hi
    lo_ref[...] = lo
    ring.finish()


def second_factor(schur, own):
    n = schur.shape[0]
    vmem = pl.BlockSpec(memory_space=pltpu.VMEM)
    shapes = [(n, n), (n, n), (ZS, 2, *own.shape)]
    return pl.pallas_call(
        second_kernel,
        out_shape=[jax.ShapeDtypeStruct(s, BF16) for s in shapes],
        in_specs=[vmem] * 2,
        out_specs=[vmem] * 3,
        scratch_shapes=[
            pltpu.VMEM((n, n), F32),
            *factor_scratch(n),
            pltpu.SemaphoreType.DMA((15,)),
            pltpu.SemaphoreType.DMA((15,)),
        ],
        compiler_params=pltpu.CompilerParams(
            vmem_limit_bytes=48 << 20, collective_id=1, has_side_effects=True
        ),
        cost_estimate=pl.CostEstimate(flops=4_000_000_000, bytes_accessed=8 << 20, transcendentals=0),
    )(schur, own)


def on_device(lead, panel, row_present, trailing):
    half = lead.shape[2] // 2
    rows_n, cols_n = lax.axis_size("row"), lax.axis_size("col")
    row_id, col_id = lax.axis_index("row"), lax.axis_index("col")
    count = panel.shape[0]
    first_row = (row_id * cols_n + col_id) * count
    tile_of = (first_row + jnp.arange(count, dtype=jnp.int32)) // TILE
    hits = tile_of[:, None] == jnp.arange(row_present.shape[0], dtype=jnp.int32)[None, :]
    present = jnp.sum(jnp.where(hits, row_present[None, :], 0), axis=1).astype(F32)
    masked = panel * present[:, None]
    per_col = trailing.shape[1] // count
    pairs = []
    for r in range(rows_n):
        for c in range(cols_n):
            pairs.append((c * per_col + r, r * cols_n + c))

    hi, lo = split_outside(masked)
    pieces = jnp.stack([hi, lo])
    row_pieces = lax.all_gather(pieces, "col", axis=1, tiled=True)
    mine = jnp.concatenate([hi[:, :half], lo[:, :half], hi[:, half:], lo[:, half:]], axis=0)
    mine = lax.ppermute(mine, ("row", "col"), pairs)
    *x1_parts, coupling, schur = lead_factor(lead)
    *x2_parts, col_pieces = second_factor(schur, mine)
    col_pieces = col_pieces.reshape(rows_n, 4, count, half)
    col_parts = [col_pieces[:, n].reshape(rows_n * count, half) for n in range(4)]

    def solve(left_hi, left_lo, right_hi, right_lo):
        first = dot3((left_hi, left_lo), x1_parts, NT).astype(BF16)
        whole = right_hi.astype(F32) + right_lo.astype(F32)
        rest = split_outside(whole - dot(first, coupling, NT))
        second = dot3(rest, x2_parts, NT).astype(BF16)
        return jnp.concatenate([first, second], axis=1)

    row_hi, row_lo = row_pieces
    rows_all = solve(row_hi[:, :half], row_lo[:, :half], row_hi[:, half:], row_lo[:, half:])
    cols_all = solve(*col_parts)
    updated = trailing - dot(rows_all, cols_all, NT)
    factor_rows = lax.dynamic_slice_in_dim(rows_all, col_id * count, count, 0)
    return (updated, factor_rows)


def solution(mesh):
    in_specs = (P(None, "row", None), P(("row", "col"), None), P(), P("row", "col"))
    out_specs = (P("row", "col"), P(("row", "col"), None))
    return jax.shard_map(
        on_device, mesh=mesh, in_specs=in_specs, out_specs=out_specs, check_vma=False
    )
```

time: 305 us -> 185 us (0.61)
  the two profiles are of different devices: /device:TPU:1 before, /device:TPU:2 now
where the time goes in v3:
time: 185 us
  Pallas kernels  128 us (69%)
  matrix products  15.9 us (9%)
  between operations  14.3 us (8%)
  local copies, waits for them, and re-layouts  12.3 us (7%)
  starting transfers between devices  10.9 us (6%)
  other arithmetic  3.35 us (2%)
    pallas_call x1, Pallas kernels, lead_factor(): pl.pallas_call(lead_kernel, out_shape=[jax.ShapeDtypeStruct(s, t) for s,...  84.6 us
    pallas_call x1, Pallas kernels, second_factor(): pl.pallas_call(second_kernel, out_shape=[jax.ShapeDtypeStruct(s, BF16) fo...  43.4 us
    dot_general x15, matrix products, dot(): return lax.dot_general(a, b, dims, preferred_element_type=F32)  15.9 us
    ppermute x1, starting transfers between devices, on_device(): mine = lax.ppermute(mine, ('row', 'col'), pairs)  10.9 us
    unnamed x26, local copies, waits for them, and re-layouts  7.3 us
  transfers between devices with their start and end apart: 2, of which 0 were waited for; matrix products, arithmetic and copies ran while one was open for 4% of the time, Pallas kernels for 69%

profile of v3, /device:TPU:2, one launch (start us, length us, event | category | flops | bytes accessed | tf_op | source)
XLA Modules:
  0.0 184.8 jit_solution(14769876721196741042)
XLA Ops:
  7.2 0.0 all-gather.2.cloned.1.call-start
  7.2 0.8 select_reduce_fusion
  8.1 1.0 reduce-precision_convert_fusion.6
  9.1 0.7 pad_maximum_fusion.4
  9.7 0.0 all-gather.2.cloned.1.call-update
  9.8 10.9 %collective-permute-start = (bf16[64,1024]{1,0:T(8,128)(2,1)S(1)}, bf16[64,1024]{1,0:T(8,128)(2,1)S(1)}, u32[]{:S(2)}, u32[]{:S(2)}) collective-permute-start(bf16[64,1024]{1,0:T(8,128)(2,1)S(1)} %pad_maximum_fusion.5), channel_id=1, source_target_pairs={{0,0},{16,1},{32,2},{48,3},{64,4},{80,5},{96,6},{112,7},{128,8},{1... | collective-permute-start | bytes 393224 | tf_op jit(solution)/shard_map/ppermute | solution.py:341
  20.7 0.0 copy-start.8
  20.7 1.0 copy-done.8
  21.8 84.6 %shard_map.59 = (bf16[1024,1024]{1,0:T(8,128)(2,1)S(1)}, bf16[1024,1024]{1,0:T(8,128)(2,1)S(1)}, bf16[1024,1024]{1,0:T(8,128)(2,1)}, f32[1024,1024]{1,0:T(8,128)}) custom-call(bf16[2,64,2048]{2,1,0:T(8,128)(2,1)S(1)} %copy-done.8), custom_call_target="tpu_custom_call" | custom-call | flops 6000000000 | bytes 16777216 | tf_op jit(solution)/shard_map/pallas_call | solution.py:264
  106.3 1.3 copy-done
  107.7 1.3 copy-done.3
  109.0 0.0 collective-permute-done.own_ref
  109.0 43.4 %shard_map.60 = (bf16[1024,1024]{1,0:T(8,128)(2,1)S(1)}, bf16[1024,1024]{1,0:T(8,128)(2,1)S(1)}, bf16[8,2,64,1024]{3,2,1,0:T(8,128)(2,1)}) custom-call(f32[1024,1024]{1,0:T(8,128)} %get-tuple-element.12.schur_ref, bf16[64,1024]{1,0:T(8,128)(2,1)S(1)} %collective-permute-done.own_ref), custom_call_target="tpu_custom_call" | custom-call | flops 4000000000 | bytes 8388608 | tf_op jit(solution)/shard_map/pallas_call | solution.py:303
  152.5 0.0 copy-start.6
  152.5 0.0 copy-start.11
  152.5 0.0 copy-start.1
  152.5 2.1 %fusion.23 = (bf16[16,1,16,1024]{3,2,1,0:T(8,128)(2,1)S(1)}, bf16[16,1,16,1024]{3,2,1,0:T(8,128)(2,1)S(1)}) fusion(bf16[16,4,16,1024]{3,2,1,0:T(8,128)(2,1)} %bitcast.32), kind=kLoop, calls=%fused_computation.48 | loop fusion | bytes 2097152 | tf_op jit(solution)/shard_map/slice | solution.py:345
  154.6 0.5 copy-done.11
  155.2 0.2 convert_add_fusion
  155.3 0.0 copy-start.4
  155.4 0.4 copy-done.1
  155.8 0.7 fusion.26
  156.5 0.5 copy-done.4
  157.0 0.7 fusion.27
  157.8 0.0 copy-start.9
  157.8 0.7 fusion.3
  158.6 0.8 copy-done.9
  159.4 0.7 convolution_subtract_fusion
  160.1 0.7 fusion.17
  160.9 0.8 convolution_add_fusion
  161.7 0.8 fusion.4
  162.4 0.0 all-gather.2.cloned.1.call-done
  162.4 0.0 copy-start.2
  162.5 2.9 %slice_bitcast_fusion = (bf16[512,2048]{1,0:T(8,128)(2,1)S(1)}, bf16[512,2048]{1,0:T(8,128)(2,1)S(1)}) fusion(bf16[2,512,2048]{2,1,0:T(8,128)(2,1)} %all-gather.2.cloned.1.call-done), kind=kLoop, calls=%fused_computation.7 | loop fusion | bytes 8388608 | tf_op jit(solution)/shard_map/unstack | solution.py:354
  165.4 1.3 fusion.15
  166.7 0.3 copy-done.5
  166.9 1.3 fusion.13
  168.3 1.3 add_convert_fusion.1
  169.6 0.3 copy-done.10
  169.8 1.3 add_subtract_fusion
  171.2 1.3 fusion.7
  172.5 0.3 copy-done.7
  172.8 1.3 fusion.19
  174.1 1.3 add_convert_fusion
  175.4 0.0 copy-start.12
  175.4 0.6 fusion.21
  176.0 0.4 copy-done.12
  176.4 1.5 fusion.5
  (11 shorter events, 0.1 us)
Async XLA Ops:
  7.2 155.3 %all-gather.2.cloned.1.call-start = ((), (), s32[]{:S(2)}) async-start(), calls=%async_computation | async-start | bytes 4325376 | tf_op jit(solution)/shard_map/all_gather | solution.py:339
  9.8 99.2 %collective-permute-start = (bf16[64,1024]{1,0:T(8,128)(2,1)S(1)}, bf16[64,1024]{1,0:T(8,128)(2,1)S(1)}, u32[]{:S(2)}, u32[]{:S(2)}) collective-permute-start(bf16[64,1024]{1,0:T(8,128)(2,1)S(1)} %pad_maximum_fusion.5), channel_id=1, source_target_pairs={{0,0},{16,1},{32,2},{48,3},{64,4},{80,5},{96,6},{112,7},{128,8},{1... | collective-permute-start | bytes 393224 | tf_op jit(solution)/shard_map/ppermute | solution.py:341
  20.7 1.0 copy-start.8
  106.3 1.3 copy-start
  107.7 1.3 copy-start.3
  152.5 8.4 %copy-start.6 = (bf16[1024,1024]{1,0:T(8,128)(2,1)}, bf16[1024,1024]{1,0:T(8,128)(2,1)S(1)}, u32[]{:S(2)}) copy-start(bf16[1024,1024]{1,0:T(8,128)(2,1)S(1)} %get-tuple-element.14) | copy-start | bytes 6291460
  152.5 2.7 %copy-start.11 = (bf16[8,2,64,1024]{3,2,1,0:T(8,128)(2,1)S(1)}, bf16[8,2,64,1024]{3,2,1,0:T(8,128)(2,1)}, u32[]{:S(2)}) copy-start(bf16[8,2,64,1024]{3,2,1,0:T(8,128)(2,1)} %get-tuple-element.15) | copy-start | bytes 6291460
  152.5 3.3 %copy-start.1 = (bf16[1024,1024]{1,0:T(8,128)(2,1)S(1)}, bf16[1024,1024]{1,0:T(8,128)(2,1)}, u32[]{:S(2)}) copy-start(bf16[1024,1024]{1,0:T(8,128)(2,1)} %copy-done) | copy-start | bytes 6291460
  155.3 1.7 copy-start.4
  157.8 1.6 copy-start.9
  162.4 2.9 %copy-start.2 = (bf16[1024,1024]{1,0:T(8,128)(2,1)S(1)}, bf16[1024,1024]{1,0:T(8,128)(2,1)}, u32[]{:S(2)}) copy-start(bf16[1024,1024]{1,0:T(8,128)(2,1)} %copy-done) | copy-start | bytes 6291460
  165.3 1.6 copy-start.5
  168.3 1.6 copy-start.10
  171.2 1.6 copy-start.7
  175.4 1.1 copy-start.12
Sparse Core Ops, SparseCore 0:
  11.7 90.4 all-gather.1

commit v4 on v3

--- a/solution.py
+++ b/solution.py
@@ -216,25 +216,24 @@
     return barrier
 
 
-def lead_kernel(lead_ref, hi_ref, lo_ref, coupling_ref, schur_ref, buf, work, *scratch):
+def lead_kernel(lead_ref, hi_ref, lo_ref, coupling_ref, buf, work, *scratch):
     factor_refs, (send_sem, recv_sem) = scratch[:5], scratch[5:]
     z, core = neighbours()[:2]
     half = lead_ref.shape[2] // 2
     barrier = greet()
     buf[0, z, core] = lead_ref[0, :, :half]
     buf[1, z, core] = lead_ref[1, :, :half]
-    buf[2, z, core] = lead_ref[1, :, half:]
     pl.semaphore_wait(barrier, 3)
 
-    first = Ring(lambda b, c: buf.at[pl.ds(0, 1), b, c], send_sem.at[0], recv_sem.at[0])
-    rest = Ring(lambda b, c: buf.at[pl.ds(1, 2), b, c], send_sem.at[1], recv_sem.at[1])
+    first = Ring(lambda b, c: buf.at[0, b, c], send_sem.at[0], recv_sem.at[0])
+    rest = Ring(lambda b, c: buf.at[1, b, c], send_sem.at[1], recv_sem.at[1])
     first.begin()
     for n in range(4):
         first.advance(n)
     rest.begin()
     first.finish()
     work[...] = buf[0].reshape(work.shape).astype(F32)
-    invert_in_place(work, *factor_refs, before=rest.advance_at((2, 4, 5, 7)))
+    invert_in_place(work, *factor_refs, before=rest.advance_at((2, 3, 5, 6)))
     hi, lo = split(work[...])
     hi_ref[...] = hi
     lo_ref[...] = lo
@@ -247,27 +246,19 @@
         left = buf[1, :, :, :, :depth].reshape(half, depth)
         coupling_ref[:, at] = (dot(left, hi_ref[at, :depth], NT) + dot(left, lo_ref[at, :depth], NT)).astype(BF16)
 
-    def schur_columns(n, carry):
-        at = pl.ds(pl.multiple_of(n * wide, wide), wide)
-        block = buf[2, :, :, :, at].reshape(half, wide).astype(F32)
-        schur_ref[:, at] = block - dot(coupling_ref[...], coupling_ref[at, :], NT)
-        return carry
-
-    lax.fori_loop(0, half // wide, schur_columns, 0)
-
 
 def lead_factor(lead):
     half = lead.shape[2] // 2
     square = (half, half)
     vmem = pl.BlockSpec(memory_space=pltpu.VMEM)
-    shapes = [(square, BF16)] * 3 + [(square, F32)]
+    shapes = [(square, BF16)] * 3
     return pl.pallas_call(
         lead_kernel,
         out_shape=[jax.ShapeDtypeStruct(s, t) for s, t in shapes],
         in_specs=[vmem],
-        out_specs=[vmem] * 4,
+        out_specs=[vmem] * 3,
         scratch_shapes=[
-            pltpu.VMEM((3, ZS, 2, half // 16, half), BF16),
+            pltpu.VMEM((2, ZS, 2, half // 16, half), BF16),
             pltpu.VMEM(square, F32),
             *factor_scratch(half),
             pltpu.SemaphoreType.DMA((2, 15)),
@@ -280,15 +271,22 @@
     )(lead)
 
 
-def second_kernel(schur_ref, own_ref, hi_ref, lo_ref, cols_ref, work, *scratch):
+def second_kernel(corner_ref, coupling_ref, own_ref, hi_ref, lo_ref, cols_ref, work, *scratch):
     factor_refs, (send_sem, recv_sem) = scratch[:5], scratch[5:]
     z, core = neighbours()[:2]
     barrier = greet()
     cols_ref[z, core] = own_ref[...]
-    work[...] = schur_ref[...]
     pl.semaphore_wait(barrier, 3)
     ring = Ring(lambda b, c: cols_ref.at[b, c], send_sem, recv_sem)
     ring.begin()
+    wide = 256
+
+    def schur_columns(n, carry):
+        at = pl.ds(pl.multiple_of(n * wide, wide), wide)
+        work[:, at] = corner_ref[:, at].astype(F32) - dot(coupling_ref[...], coupling_ref[at, :], NT)
+        return carry
+
+    lax.fori_loop(0, work.shape[0] // wide, schur_columns, 0)
     invert_in_place(work, *factor_refs, before=ring.advance_at((1, 2, 3, 4)))
     hi, lo = split(work[...])
     hi_ref[...] = hi
@@ -296,14 +294,14 @@
     ring.finish()
 
 
-def second_factor(schur, own):
-    n = schur.shape[0]
+def second_factor(corner, coupling, own):
+    n = corner.shape[0]
     vmem = pl.BlockSpec(memory_space=pltpu.VMEM)
     shapes = [(n, n), (n, n), (ZS, 2, *own.shape)]
     return pl.pallas_call(
         second_kernel,
         out_shape=[jax.ShapeDtypeStruct(s, BF16) for s in shapes],
-        in_specs=[vmem] * 2,
+        in_specs=[vmem] * 3,
         out_specs=[vmem] * 3,
         scratch_shapes=[
             pltpu.VMEM((n, n), F32),
@@ -315,13 +313,14 @@
             vmem_limit_bytes=48 << 20, collective_id=1, has_side_effects=True
         ),
         cost_estimate=pl.CostEstimate(flops=4_000_000_000, bytes_accessed=8 << 20, transcendentals=0),
-    )(schur, own)
+    )(corner, coupling, own)
 
 
 def on_device(lead, panel, row_present, trailing):
     half = lead.shape[2] // 2
     rows_n, cols_n = lax.axis_size("row"), lax.axis_size("col")
     row_id, col_id = lax.axis_index("row"), lax.axis_index("col")
+    corner = lax.all_gather(lead[1, :, half:], "row", axis=0, tiled=True)
     count = panel.shape[0]
     first_row = (row_id * cols_n + col_id) * count
     tile_of = (first_row + jnp.arange(count, dtype=jnp.int32)) // TILE
@@ -335,12 +334,11 @@
             pairs.append((c * per_col + r, r * cols_n + c))
 
     hi, lo = split_outside(masked)
-    pieces = jnp.stack([hi, lo])
-    row_pieces = lax.all_gather(pieces, "col", axis=1, tiled=True)
-    mine = jnp.concatenate([hi[:, :half], lo[:, :half], hi[:, half:], lo[:, half:]], axis=0)
-    mine = lax.ppermute(mine, ("row", "col"), pairs)
-    *x1_parts, coupling, schur = lead_factor(lead)
-    *x2_parts, col_pieces = second_factor(schur, mine)
+    four = [hi[:, :half], lo[:, :half], hi[:, half:], lo[:, half:]]
+    row_pieces = lax.all_gather(jnp.stack(four), "col", axis=1, tiled=True)
+    mine = lax.ppermute(jnp.concatenate(four, axis=0), ("row", "col"), pairs)
+    *x1_parts, coupling = lead_factor(lead)
+    *x2_parts, col_pieces = second_factor(corner, coupling, mine)
     col_pieces = col_pieces.reshape(rows_n, 4, count, half)
     col_parts = [col_pieces[:, n].reshape(rows_n * count, half) for n in range(4)]
 
@@ -351,8 +349,7 @@
         second = dot3(rest, x2_parts, NT).astype(BF16)
         return jnp.concatenate([first, second], axis=1)
 
-    row_hi, row_lo = row_pieces
-    rows_all = solve(row_hi[:, :half], row_lo[:, :half], row_hi[:, half:], row_lo[:, half:])
+    rows_all = solve(*[row_pieces[n] for n in range(4)])
     cols_all = solve(*col_parts)
     updated = trailing - dot(rows_all, cols_all, NT)
     factor_rows = lax.dynamic_slice_in_dim(rows_all, col_id * count, count, 0)

time: 185 us -> 191 us (1.032)
  Pallas kernels: 128 us -> 133 us
  local copies, waits for them, and re-layouts: 12.3 us -> 9.08 us
  other arithmetic: 3.35 us -> 5.35 us
    pallas_call x1, Pallas kernels: 43.4 us -> 46.3 us  [second_factor(): pl.pallas_call(second_kernel, out_shape=[jax.ShapeDtypeStruct(s, BF16) fo...]
    another operation x1, local copies, waits for them, and re-layouts: 2.87 us -> 0.02 us  [on_device(): row_pieces = lax.all_gather(jnp.stack(four), 'col', axis=1, tiled=True)]
    pallas_call x1, Pallas kernels: 84.6 us -> 86.7 us  [lead_factor(): pl.pallas_call(lead_kernel, out_shape=[jax.ShapeDtypeStruct(s, t) for s,...]
    slice x1, local copies, waits for them, and re-layouts: 2.1 us -> 0.1 us  [on_device(): col_pieces[:, n].reshape(rows_n * count, half)]
    add x1, other arithmetic: 0.18 us -> 2.17 us  [solve(): whole = right_hi.astype(F32) + right_lo.astype(F32)]
    dot_general x15, matrix products: 15.9 us -> 17.8 us  [dot(): return lax.dot_general(a, b, dims, preferred_element_type=F32)]
  transfers between devices with their start and end apart: 2 -> 3, of which waited for: 0 -> 0; matrix products, arithmetic and copies ran while one was open for 4% -> 5% of each run, Pallas kernels for 69% -> 70%
where the time goes in v4:
time: 191 us
  Pallas kernels  133 us (70%)
  matrix products  17.8 us (9%)
  between operations  14.3 us (7%)
  starting transfers between devices  11 us (6%)
  local copies, waits for them, and re-layouts  9.08 us (5%)
  other arithmetic  5.35 us (3%)
    pallas_call x1, Pallas kernels, lead_factor(): pl.pallas_call(lead_kernel, out_shape=[jax.ShapeDtypeStruct(s, t) for s,...  86.7 us
    pallas_call x1, Pallas kernels, second_factor(): pl.pallas_call(second_kernel, out_shape=[jax.ShapeDtypeStruct(s, BF16) fo...  46.3 us
    dot_general x15, matrix products, dot(): return lax.dot_general(a, b, dims, preferred_element_type=F32)  17.8 us
    ppermute x1, starting transfers between devices, on_device(): mine = lax.ppermute(jnp.concatenate(four, axis=0), ('row', 'col'), pairs)  10.9 us
    unnamed x26, local copies, waits for them, and re-layouts  7.39 us
  transfers between devices with their start and end apart: 3, of which 0 were waited for; matrix products, arithmetic and copies ran while one was open for 5% of the time, Pallas kernels for 70%

profile of v4, /device:TPU:2, one launch (start us, length us, event | category | flops | bytes accessed | tf_op | source)
XLA Modules:
  0.0 190.6 jit_solution(15807469005171529436)
XLA Ops:
  7.2 0.0 all-gather.6.cloned.1.call-start
  7.2 1.6 slice.47
  8.8 0.0 all-gather.6.cloned.1.call-update
  8.8 0.0 all-gather.4.cloned.1.call-start
  8.9 0.8 select_reduce_fusion
  9.7 1.0 reduce-precision_convert_fusion.6
  10.8 0.7 pad_maximum_fusion.4
  11.4 0.0 all-gather.4.cloned.1.call-update
  11.5 10.9 %collective-permute-start = (bf16[64,1024]{1,0:T(8,128)(2,1)S(1)}, bf16[64,1024]{1,0:T(8,128)(2,1)S(1)}, u32[]{:S(2)}, u32[]{:S(2)}) collective-permute-start(bf16[64,1024]{1,0:T(8,128)(2,1)S(1)} %pad_maximum_fusion.5), channel_id=1, source_target_pairs={{0,0},{16,1},{32,2},{48,3},{64,4},{80,5},{96,6},{112,7},{128,8},{1... | collective-permute-start | bytes 393224 | tf_op jit(solution)/shard_map/ppermute | solution.py:339
  22.4 0.0 copy-start.7
  22.4 1.0 copy-done.7
  23.4 86.7 %shard_map.59 = (bf16[1024,1024]{1,0:T(8,128)(2,1)S(1)}, bf16[1024,1024]{1,0:T(8,128)(2,1)S(1)}, bf16[1024,1024]{1,0:T(8,128)(2,1)}) custom-call(bf16[2,64,2048]{2,1,0:T(8,128)(2,1)S(1)} %copy-done.7), custom_call_target="tpu_custom_call" | custom-call | flops 6000000000 | bytes 16777216 | tf_op jit(solution)/shard_map/pallas_call | solution.py:255
  110.1 0.0 copy-start
  110.1 1.4 copy-done
  111.5 1.3 copy-done.3
  112.8 0.0 collective-permute-done.own_ref
  112.8 46.3 %shard_map.60 = (bf16[1024,1024]{1,0:T(8,128)(2,1)S(1)}, bf16[1024,1024]{1,0:T(8,128)(2,1)S(1)}, bf16[8,2,64,1024]{3,2,1,0:T(8,128)(2,1)}) custom-call(bf16[1024,1024]{1,0:T(8,128)(2,1)} %bitcast.47, bf16[1024,1024]{1,0:T(8,128)(2,1)} %get-tuple-element.10.coupling_ref, bf16[64,1024]{1,0:T(8,128)(2,1)S(1)} %collective-permute-done.own_ref), custom_call_target="tpu_custom_call" | custom-call | flops 4000000000 | bytes 8388608 | tf_op jit(solution)/shard_map/pallas_call | solution.py:301
  159.1 0.0 copy-start.5
  159.1 0.0 copy-start.10
  159.2 2.2 %convert_add_fusion = f32[16,1,16,1024]{3,2,1,0:T(8,128)S(1)} fusion(bf16[16,4,16,1024]{3,2,1,0:T(8,128)(2,1)} %bitcast.44), kind=kLoop, calls=%fused_computation.27 | loop fusion | flops 786432 | bytes 2097152 | tf_op jit(solution)/shard_map/add | solution.py:347
  161.3 0.5 copy-done.10
  161.8 0.1 fusion.20
  161.9 0.5 copy-done.4
  162.4 0.7 fusion.22
  163.2 0.5 copy-done.1
  163.6 0.7 fusion.21
  164.4 0.7 fusion.3
  165.1 0.8 copy-done.8
  166.0 0.7 convolution_subtract_fusion
  166.7 0.7 fusion.14
  167.5 0.7 convolution_add_fusion
  168.2 0.8 fusion.4
  169.0 0.0 all-gather.4.cloned.1.call-done
  169.0 3.3 %fusion.12 = f32[512,1024]{1,0:T(8,128)S(1)} fusion(bf16[1024,1024]{1,0:T(8,128)(2,1)} %copy-done.3, bf16[4,512,1024]{2,1,0:T(8,128)(2,1)} %all-gather.4.cloned.1.call-done), kind=kOutput, calls=%fused_computation.28 | convolution fusion | flops 1073741824 | bytes 5242880 | tf_op jit(solution)/shard_map/dot_general | solution.py:87
  172.4 0.0 copy-done.2
  172.4 0.4 copy-done.11
  172.8 1.3 fusion.13
  174.1 1.3 add_convert_fusion.1
  175.4 0.3 copy-done.9
  175.7 1.3 bitcast_subtract_fusion
  177.0 0.3 copy-done.6
  177.3 1.3 fusion.16
  178.6 1.3 fusion.7
  179.9 1.3 add_convert_fusion
  181.2 0.0 copy-start.12
  181.2 0.6 fusion.18
  181.8 0.4 copy-done.12
  182.2 1.5 fusion.5
  (14 shorter events, 0.1 us)
Async XLA Ops:
  7.2 105.6 %all-gather.6.cloned.1.call-start = ((), (), s32[]{:S(2)}) async-start(), calls=%async_computation.1 | async-start | bytes 2228224 | tf_op jit(solution)/shard_map/all_gather | solution.py:323
  8.8 160.2 %all-gather.4.cloned.1.call-start = ((), (), s32[]{:S(2)}) async-start(), calls=%async_computation | async-start | bytes 4325376 | tf_op jit(solution)/shard_map/all_gather | solution.py:338
  11.5 101.3 %collective-permute-start = (bf16[64,1024]{1,0:T(8,128)(2,1)S(1)}, bf16[64,1024]{1,0:T(8,128)(2,1)S(1)}, u32[]{:S(2)}, u32[]{:S(2)}) collective-permute-start(bf16[64,1024]{1,0:T(8,128)(2,1)S(1)} %pad_maximum_fusion.5), channel_id=1, source_target_pairs={{0,0},{16,1},{32,2},{48,3},{64,4},{80,5},{96,6},{112,7},{128,8},{1... | collective-permute-start | bytes 393224 | tf_op jit(solution)/shard_map/ppermute | solution.py:339
  22.4 1.0 copy-start.7
  110.1 1.4 copy-start
  111.5 1.3 copy-start.3
  159.1 8.4 %copy-start.5 = (bf16[1024,1024]{1,0:T(8,128)(2,1)}, bf16[1024,1024]{1,0:T(8,128)(2,1)S(1)}, u32[]{:S(2)}) copy-start(bf16[1024,1024]{1,0:T(8,128)(2,1)S(1)} %get-tuple-element.12) | copy-start | bytes 6291460
  159.1 2.7 %copy-start.10 = (bf16[8,2,64,1024]{3,2,1,0:T(8,128)(2,1)S(1)}, bf16[8,2,64,1024]{3,2,1,0:T(8,128)(2,1)}, u32[]{:S(2)}) copy-start(bf16[8,2,64,1024]{3,2,1,0:T(8,128)(2,1)} %get-tuple-element.13) | copy-start | bytes 6291460
  159.1 3.3 %copy-start.4 = (bf16[1024,1024]{1,0:T(8,128)(2,1)S(1)}, bf16[1024,1024]{1,0:T(8,128)(2,1)}, u32[]{:S(2)}) copy-start(bf16[1024,1024]{1,0:T(8,128)(2,1)} %copy-done.3) | copy-start | bytes 6291460
  161.9 1.7 copy-start.1
  164.4 1.6 copy-start.8
  169.0 3.4 %copy-start.2 = (bf16[1024,1024]{1,0:T(8,128)(2,1)S(1)}, bf16[1024,1024]{1,0:T(8,128)(2,1)}, u32[]{:S(2)}) copy-start(bf16[1024,1024]{1,0:T(8,128)(2,1)} %copy-done) | copy-start | bytes 6291460
  169.0 3.8 %copy-start.11 = (bf16[4,512,1024]{2,1,0:T(8,128)(2,1)S(1)}, bf16[4,512,1024]{2,1,0:T(8,128)(2,1)}, u32[]{:S(2)}) copy-start(bf16[4,512,1024]{2,1,0:T(8,128)(2,1)} %all-gather.4.cloned.1.call-done) | copy-start | bytes 12582916
  174.1 1.6 copy-start.9
  175.7 1.6 copy-start.6
  181.2 1.1 copy-start.12
Sparse Core Ops, SparseCore 0:
  10.7 54.2 all-gather.5
  68.2 81.6 all-gather.3

commit v5 on v3

--- a/solution.py
+++ b/solution.py
@@ -282,18 +282,64 @@
 
 def second_kernel(schur_ref, own_ref, hi_ref, lo_ref, cols_ref, work, *scratch):
     factor_refs, (send_sem, recv_sem) = scratch[:5], scratch[5:]
-    z, core = neighbours()[:2]
+    row, col = lax.axis_index("row"), lax.axis_index("col")
+    rows_n, cols_n = lax.axis_size("row"), lax.axis_size("col")
+    z, core = row // 2, row % 2
+    flat, from_flat = row * cols_n + col, col * rows_n + row
+    to_row, to_col = flat % rows_n, flat // rows_n
+    moves = (to_row != row) | (to_col != col)
     barrier = greet()
-    cols_ref[z, core] = own_ref[...]
+
+    @pl.when(moves)
+    def _():
+        for peer in ((to_row, to_col), (from_flat // cols_n, from_flat % cols_n)):
+            pl.semaphore_signal(barrier, inc=1, device_id=peer, device_id_type=MESH)
+
     work[...] = schur_ref[...]
-    pl.semaphore_wait(barrier, 3)
+
+    def shift():
+        return pltpu.make_async_remote_copy(
+            src_ref=own_ref,
+            dst_ref=cols_ref.at[to_row // 2, to_row % 2],
+            send_sem=send_sem.at[15],
+            recv_sem=recv_sem.at[15],
+            device_id=(to_row, to_col),
+            device_id_type=MESH,
+        )
+
+    @pl.when(moves)
+    def _():
+        pl.semaphore_wait(barrier, 5)
+        shift().start()
+
+    @pl.when(jnp.logical_not(moves))
+    def _():
+        pl.semaphore_wait(barrier, 3)
+        cols_ref[z, core] = own_ref[...]
+
     ring = Ring(lambda b, c: cols_ref.at[b, c], send_sem, recv_sem)
-    ring.begin()
-    invert_in_place(work, *factor_refs, before=ring.advance_at((1, 2, 3, 4)))
+    later = ring.advance_at((4, 5, 6, 7))
+
+    def before(j):
+        @pl.when((j == 3) & moves)
+        def _():
+            shift().wait_recv()
+
+        @pl.when(j == 3)
+        def _():
+            ring.begin()
+
+        later(j)
+
+    invert_in_place(work, *factor_refs, before=before)
     hi, lo = split(work[...])
     hi_ref[...] = hi
     lo_ref[...] = lo
     ring.finish()
+
+    @pl.when(moves)
+    def _():
+        shift().wait_send()
 
 
 def second_factor(schur, own):
@@ -308,8 +354,8 @@
         scratch_shapes=[
             pltpu.VMEM((n, n), F32),
             *factor_scratch(n),
-            pltpu.SemaphoreType.DMA((15,)),
-            pltpu.SemaphoreType.DMA((15,)),
+            pltpu.SemaphoreType.DMA((16,)),
+            pltpu.SemaphoreType.DMA((16,)),
         ],
         compiler_params=pltpu.CompilerParams(
             vmem_limit_bytes=48 << 20, collective_id=1, has_side_effects=True
@@ -328,19 +374,11 @@
     hits = tile_of[:, None] == jnp.arange(row_present.shape[0], dtype=jnp.int32)[None, :]
     present = jnp.sum(jnp.where(hits, row_present[None, :], 0), axis=1).astype(F32)
     masked = panel * present[:, None]
-    per_col = trailing.shape[1] // count
-    pairs = []
-    for r in range(rows_n):
-        for c in range(cols_n):
-            pairs.append((c * per_col + r, r * cols_n + c))
-
     hi, lo = split_outside(masked)
-    pieces = jnp.stack([hi, lo])
-    row_pieces = lax.all_gather(pieces, "col", axis=1, tiled=True)
-    mine = jnp.concatenate([hi[:, :half], lo[:, :half], hi[:, half:], lo[:, half:]], axis=0)
-    mine = lax.ppermute(mine, ("row", "col"), pairs)
+    four = [hi[:, :half], lo[:, :half], hi[:, half:], lo[:, half:]]
+    row_pieces = lax.all_gather(jnp.stack(four), "col", axis=1, tiled=True)
     *x1_parts, coupling, schur = lead_factor(lead)
-    *x2_parts, col_pieces = second_factor(schur, mine)
+    *x2_parts, col_pieces = second_factor(schur, jnp.concatenate(four, axis=0))
     col_pieces = col_pieces.reshape(rows_n, 4, count, half)
     col_parts = [col_pieces[:, n].reshape(rows_n * count, half) for n in range(4)]
 
@@ -351,8 +389,7 @@
         second = dot3(rest, x2_parts, NT).astype(BF16)
         return jnp.concatenate([first, second], axis=1)
 
-    row_hi, row_lo = row_pieces
-    rows_all = solve(row_hi[:, :half], row_lo[:, :half], row_hi[:, half:], row_lo[:, half:])
+    rows_all = solve(*[row_pieces[n] for n in range(4)])
     cols_all = solve(*col_parts)
     updated = trailing - dot(rows_all, cols_all, NT)
     factor_rows = lax.dynamic_slice_in_dim(rows_all, col_id * count, count, 0)

time: 185 us -> 176 us (0.951)
  the two profiles are of different devices: /device:TPU:2 before, /device:TPU:1 now
where the time goes in v5:
time: 176 us; the launch traced here: 174 us
  Pallas kernels  132 us (75%)
  matrix products  17.2 us (10%)
  between operations  14.3 us (8%)
  local copies, waits for them, and re-layouts  7.03 us (4%)
  other arithmetic  3.36 us (2%)
    pallas_call x1, Pallas kernels, lead_factor(): pl.pallas_call(lead_kernel, out_shape=[jax.ShapeDtypeStruct(s, t) for s,...  81.5 us
    pallas_call x1, Pallas kernels, second_factor(): pl.pallas_call(second_kernel, out_shape=[jax.ShapeDtypeStruct(s, BF16) fo...  50.1 us
    dot_general x15, matrix products, dot(): return lax.dot_general(a, b, dims, preferred_element_type=F32)  17.2 us
    unnamed x24, local copies, waits for them, and re-layouts  4.75 us
  transfers between devices with their start and end apart: 1, of which 0 were waited for; matrix products, arithmetic and copies ran while one was open for 4% of the time, Pallas kernels for 76%

profile of v5, /device:TPU:1, one launch (start us, length us, event | category | flops | bytes accessed | tf_op | source)
XLA Modules:
  0.0 173.5 jit_solution(8289128385031977626)
XLA Ops:
  7.2 0.0 all-gather.2.cloned.1.call-start
  7.2 0.8 select_reduce_fusion
  8.1 1.0 reduce-precision_convert_fusion.6
  9.1 0.7 pad_maximum_fusion.4
  9.8 0.0 all-gather.2.cloned.1.call-update
  9.8 0.0 copy-start.6
  9.8 1.0 copy-done.6
  10.9 81.5 %shard_map.59 = (bf16[1024,1024]{1,0:T(8,128)(2,1)S(1)}, bf16[1024,1024]{1,0:T(8,128)(2,1)S(1)}, bf16[1024,1024]{1,0:T(8,128)(2,1)}, f32[1024,1024]{1,0:T(8,128)}) custom-call(bf16[2,64,2048]{2,1,0:T(8,128)(2,1)S(1)} %copy-done.6), custom_call_target="tpu_custom_call" | custom-call | flops 6000000000 | bytes 16777216 | tf_op jit(solution)/shard_map/pallas_call | solution.py:264
  92.4 0.0 copy-start.2
  92.4 50.1 %shard_map.60 = (bf16[1024,1024]{1,0:T(8,128)(2,1)S(1)}, bf16[1024,1024]{1,0:T(8,128)(2,1)S(1)}, bf16[8,2,64,1024]{3,2,1,0:T(8,128)(2,1)}) custom-call(f32[1024,1024]{1,0:T(8,128)} %get-tuple-element.12.schur_ref, bf16[64,1024]{1,0:T(8,128)(2,1)S(1)} %pad_maximum_fusion.5.own_ref), custom_call_target="tpu_custom_call" | custom-call | flops 4000000000 | bytes 8388608 | tf_op jit(solution)/shard_map/pallas_call | solution.py:349
  142.5 0.0 copy-start.4
  142.5 0.0 copy-start
  142.5 0.0 copy-start.9
  142.5 2.3 %fusion.22 = (bf16[16,1,16,1024]{3,2,1,0:T(8,128)(2,1)S(1)}, bf16[16,1,16,1024]{3,2,1,0:T(8,128)(2,1)S(1)}) fusion(bf16[16,4,16,1024]{3,2,1,0:T(8,128)(2,1)} %bitcast.43), kind=kLoop, calls=%fused_computation.50 | loop fusion | bytes 2097152 | tf_op jit(solution)/shard_map/slice | solution.py:383
  144.8 1.1 copy-done.9
  145.9 0.2 convert_add_fusion
  146.1 0.7 fusion.23
  146.9 0.0 copy-done.2
  146.9 0.7 fusion.24
  147.6 0.0 copy-start.7
  147.6 0.7 fusion.4
  148.4 0.8 copy-done.7
  149.2 0.7 convolution_subtract_fusion
  150.0 0.0 copy-done.4
  150.0 0.7 fusion.17
  150.7 0.7 fusion.18
  151.5 0.0 copy-done
  151.5 0.8 fusion.5
  152.3 0.0 all-gather.2.cloned.1.call-done
  152.3 0.0 copy-start.3
  152.3 0.0 copy-start.10
  152.3 2.7 %fusion.13 = f32[512,1024]{1,0:T(8,128)S(1)} fusion(bf16[1024,1024]{1,0:T(8,128)(2,1)S(1)} %get-tuple-element.9, bf16[4,512,1024]{2,1,0:T(8,128)(2,1)} %all-gather.2.cloned.1.call-done), kind=kOutput, calls=%fused_computation.28 | convolution fusion | flops 1073741824 | bytes 5242880 | tf_op jit(solution)/shard_map/dot_general | solution.py:87
  155.0 0.0 copy-done.3
  155.0 0.4 copy-done.10
  155.4 1.3 fusion.12
  156.7 0.0 copy-start.8
  156.7 1.3 add_convert_fusion.1
  158.0 0.3 copy-done.8
  158.3 1.3 bitcast_subtract_fusion
  159.6 0.3 copy-done.5
  159.9 1.3 fusion.15
  161.2 0.3 copy-done.1
  161.5 1.3 fusion.16
  162.8 1.3 add_convert_fusion
  164.1 0.0 copy-start.11
  164.1 0.6 fusion.20
  164.7 0.4 copy-done.11
  165.2 1.5 fusion.6
  (6 shorter events, 0.1 us)
Async XLA Ops:
  7.2 145.1 %all-gather.2.cloned.1.call-start = ((), (), s32[]{:S(2)}) async-start(), calls=%async_computation | async-start | bytes 4325376 | tf_op jit(solution)/shard_map/all_gather | solution.py:379
  9.8 1.0 copy-start.6
  92.4 54.5 %copy-start.2 = (bf16[1024,1024]{1,0:T(8,128)(2,1)}, bf16[1024,1024]{1,0:T(8,128)(2,1)S(1)}, u32[]{:S(2)}) copy-start(bf16[1024,1024]{1,0:T(8,128)(2,1)S(1)} %get-tuple-element.10) | copy-start | bytes 6291460
  142.5 7.5 %copy-start.4 = (bf16[1024,1024]{1,0:T(8,128)(2,1)}, bf16[1024,1024]{1,0:T(8,128)(2,1)S(1)}, u32[]{:S(2)}) copy-start(bf16[1024,1024]{1,0:T(8,128)(2,1)S(1)} %get-tuple-element.14) | copy-start | bytes 6291460
  142.5 9.0 %copy-start = (bf16[1024,1024]{1,0:T(8,128)(2,1)}, bf16[1024,1024]{1,0:T(8,128)(2,1)S(1)}, u32[]{:S(2)}) copy-start(bf16[1024,1024]{1,0:T(8,128)(2,1)S(1)} %get-tuple-element.13) | copy-start | bytes 6291460
  142.5 3.4 %copy-start.9 = (bf16[8,2,64,1024]{3,2,1,0:T(8,128)(2,1)S(1)}, bf16[8,2,64,1024]{3,2,1,0:T(8,128)(2,1)}, u32[]{:S(2)}) copy-start(bf16[8,2,64,1024]{3,2,1,0:T(8,128)(2,1)} %get-tuple-element.15) | copy-start | bytes 6291460
  147.6 1.6 copy-start.7
  152.3 2.7 %copy-start.3 = (bf16[1024,1024]{1,0:T(8,128)(2,1)S(1)}, bf16[1024,1024]{1,0:T(8,128)(2,1)}, u32[]{:S(2)}) copy-start(bf16[1024,1024]{1,0:T(8,128)(2,1)} %copy-done.2) | copy-start | bytes 6291460
  152.3 3.1 %copy-start.10 = (bf16[4,512,1024]{2,1,0:T(8,128)(2,1)S(1)}, bf16[4,512,1024]{2,1,0:T(8,128)(2,1)}, u32[]{:S(2)}) copy-start(bf16[4,512,1024]{2,1,0:T(8,128)(2,1)} %all-gather.2.cloned.1.call-done) | copy-start | bytes 12582916
  156.7 1.6 copy-start.8
  158.3 1.6 copy-start.5
  159.9 1.6 copy-start.1
  164.1 1.1 copy-start.11
Sparse Core Ops, SparseCore 0:
  11.7 89.8 all-gather.1

commit v6 on v5

--- a/solution.py
+++ b/solution.py
@@ -318,14 +318,14 @@
         cols_ref[z, core] = own_ref[...]
 
     ring = Ring(lambda b, c: cols_ref.at[b, c], send_sem, recv_sem)
-    later = ring.advance_at((4, 5, 6, 7))
+    later = ring.advance_at((3, 4, 5, 6))
 
     def before(j):
-        @pl.when((j == 3) & moves)
+        @pl.when((j == 2) & moves)
         def _():
             shift().wait_recv()
 
-        @pl.when(j == 3)
+        @pl.when(j == 2)
         def _():
             ring.begin()
 

time: 176 us -> 176 us (level)
  no operation moved by 1% of the time
where the time goes in v6:
time: 176 us; the launch traced here: 173 us
  Pallas kernels  131 us (74%)
  matrix products  17.2 us (10%)
  between operations  14.3 us (8%)
  local copies, waits for them, and re-layouts  7.04 us (4%)
  other arithmetic  3.36 us (2%)
    pallas_call x1, Pallas kernels, lead_factor(): pl.pallas_call(lead_kernel, out_shape=[jax.ShapeDtypeStruct(s, t) for s,...  81.5 us
    pallas_call x1, Pallas kernels, second_factor(): pl.pallas_call(second_kernel, out_shape=[jax.ShapeDtypeStruct(s, BF16) fo...  49.6 us
    dot_general x15, matrix products, dot(): return lax.dot_general(a, b, dims, preferred_element_type=F32)  17.2 us
    unnamed x24, local copies, waits for them, and re-layouts  4.75 us
  transfers between devices with their start and end apart: 1, of which 0 were waited for; matrix products, arithmetic and copies ran while one was open for 4% of the time, Pallas kernels for 76%

profile of v6, /device:TPU:1, one launch (start us, length us, event | category | flops | bytes accessed | tf_op | source)
XLA Modules:
  0.0 173.1 jit_solution(4155343662921237084)
XLA Ops:
  7.2 0.0 all-gather.2.cloned.1.call-start
  7.2 0.8 select_reduce_fusion
  8.1 1.0 reduce-precision_convert_fusion.6
  9.1 0.7 pad_maximum_fusion.4
  9.8 0.0 all-gather.2.cloned.1.call-update
  9.8 0.0 copy-start.6
  9.8 1.0 copy-done.6
  10.9 81.5 %shard_map.59 = (bf16[1024,1024]{1,0:T(8,128)(2,1)S(1)}, bf16[1024,1024]{1,0:T(8,128)(2,1)S(1)}, bf16[1024,1024]{1,0:T(8,128)(2,1)}, f32[1024,1024]{1,0:T(8,128)}) custom-call(bf16[2,64,2048]{2,1,0:T(8,128)(2,1)S(1)} %copy-done.6), custom_call_target="tpu_custom_call" | custom-call | flops 6000000000 | bytes 16777216 | tf_op jit(solution)/shard_map/pallas_call | solution.py:264
  92.4 0.0 copy-start.2
  92.4 49.6 %shard_map.60 = (bf16[1024,1024]{1,0:T(8,128)(2,1)S(1)}, bf16[1024,1024]{1,0:T(8,128)(2,1)S(1)}, bf16[8,2,64,1024]{3,2,1,0:T(8,128)(2,1)}) custom-call(f32[1024,1024]{1,0:T(8,128)} %get-tuple-element.12.schur_ref, bf16[64,1024]{1,0:T(8,128)(2,1)S(1)} %pad_maximum_fusion.5.own_ref), custom_call_target="tpu_custom_call" | custom-call | flops 4000000000 | bytes 8388608 | tf_op jit(solution)/shard_map/pallas_call | solution.py:349
  142.1 0.0 copy-start.4
  142.1 0.0 copy-start
  142.1 0.0 copy-start.9
  142.1 2.3 %fusion.22 = (bf16[16,1,16,1024]{3,2,1,0:T(8,128)(2,1)S(1)}, bf16[16,1,16,1024]{3,2,1,0:T(8,128)(2,1)S(1)}) fusion(bf16[16,4,16,1024]{3,2,1,0:T(8,128)(2,1)} %bitcast.43), kind=kLoop, calls=%fused_computation.50 | loop fusion | bytes 2097152 | tf_op jit(solution)/shard_map/slice | solution.py:383
  144.4 1.1 copy-done.9
  145.5 0.2 convert_add_fusion
  145.7 0.7 fusion.23
  146.4 0.0 copy-done.2
  146.4 0.7 fusion.24
  147.2 0.0 copy-start.7
  147.2 0.7 fusion.4
  148.0 0.8 copy-done.7
  148.8 0.7 convolution_subtract_fusion
  149.5 0.0 copy-done.4
  149.6 0.7 fusion.17
  150.3 0.7 fusion.18
  151.0 0.0 copy-done
  151.1 0.7 fusion.5
  151.8 0.0 all-gather.2.cloned.1.call-done
  151.8 0.0 copy-start.3
  151.9 0.0 copy-start.10
  151.9 2.7 %fusion.13 = f32[512,1024]{1,0:T(8,128)S(1)} fusion(bf16[1024,1024]{1,0:T(8,128)(2,1)S(1)} %get-tuple-element.9, bf16[4,512,1024]{2,1,0:T(8,128)(2,1)} %all-gather.2.cloned.1.call-done), kind=kOutput, calls=%fused_computation.28 | convolution fusion | flops 1073741824 | bytes 5242880 | tf_op jit(solution)/shard_map/dot_general | solution.py:87
  154.5 0.0 copy-done.3
  154.5 0.4 copy-done.10
  155.0 1.3 fusion.12
  156.3 0.0 copy-start.8
  156.3 1.3 add_convert_fusion.1
  157.6 0.3 copy-done.8
  157.9 1.3 bitcast_subtract_fusion
  159.2 0.3 copy-done.5
  159.5 1.3 fusion.15
  160.8 0.3 copy-done.1
  161.1 1.3 fusion.16
  162.3 1.3 add_convert_fusion
  163.6 0.0 copy-start.11
  163.7 0.6 fusion.20
  164.3 0.4 copy-done.11
  164.7 1.5 fusion.6
  (6 shorter events, 0.1 us)
Async XLA Ops:
  7.2 144.7 %all-gather.2.cloned.1.call-start = ((), (), s32[]{:S(2)}) async-start(), calls=%async_computation | async-start | bytes 4325376 | tf_op jit(solution)/shard_map/all_gather | solution.py:379
  9.8 1.0 copy-start.6
  92.4 54.0 %copy-start.2 = (bf16[1024,1024]{1,0:T(8,128)(2,1)}, bf16[1024,1024]{1,0:T(8,128)(2,1)S(1)}, u32[]{:S(2)}) copy-start(bf16[1024,1024]{1,0:T(8,128)(2,1)S(1)} %get-tuple-element.10) | copy-start | bytes 6291460
  142.1 7.5 %copy-start.4 = (bf16[1024,1024]{1,0:T(8,128)(2,1)}, bf16[1024,1024]{1,0:T(8,128)(2,1)S(1)}, u32[]{:S(2)}) copy-start(bf16[1024,1024]{1,0:T(8,128)(2,1)S(1)} %get-tuple-element.14) | copy-start | bytes 6291460
  142.1 9.0 %copy-start = (bf16[1024,1024]{1,0:T(8,128)(2,1)}, bf16[1024,1024]{1,0:T(8,128)(2,1)S(1)}, u32[]{:S(2)}) copy-start(bf16[1024,1024]{1,0:T(8,128)(2,1)S(1)} %get-tuple-element.13) | copy-start | bytes 6291460
  142.1 3.4 %copy-start.9 = (bf16[8,2,64,1024]{3,2,1,0:T(8,128)(2,1)S(1)}, bf16[8,2,64,1024]{3,2,1,0:T(8,128)(2,1)}, u32[]{:S(2)}) copy-start(bf16[8,2,64,1024]{3,2,1,0:T(8,128)(2,1)} %get-tuple-element.15) | copy-start | bytes 6291460
  147.2 1.6 copy-start.7
  151.8 2.7 %copy-start.3 = (bf16[1024,1024]{1,0:T(8,128)(2,1)S(1)}, bf16[1024,1024]{1,0:T(8,128)(2,1)}, u32[]{:S(2)}) copy-start(bf16[1024,1024]{1,0:T(8,128)(2,1)} %copy-done.2) | copy-start | bytes 6291460
  151.9 3.1 %copy-start.10 = (bf16[4,512,1024]{2,1,0:T(8,128)(2,1)S(1)}, bf16[4,512,1024]{2,1,0:T(8,128)(2,1)}, u32[]{:S(2)}) copy-start(bf16[4,512,1024]{2,1,0:T(8,128)(2,1)} %all-gather.2.cloned.1.call-done) | copy-start | bytes 12582916
  156.3 1.6 copy-start.8
  157.9 1.6 copy-start.5
  159.5 1.6 copy-start.1
  163.6 1.1 copy-start.11
Sparse Core Ops, SparseCore 0:
  11.7 89.8 all-gather.1
